TPU v7x, 32 devices: a whole 2x2x4 slice. The times are simulated.
32 devices in a mesh: branch: 2 (over x), rows: 16 (over z, y, core).
Axes of the slice: x: 2, y: 2, z: 4, core: 2. Of those that a mesh axis runs over, the one named last changes fastest.
Arguments:
- inputs: bfloat16 [16, 1024, 1024], P('rows', 'branch'), may hold values from -6 to 6
- lengths: int32 [16, 8], P('rows'), may hold values from 1 to 512, as said below
- norm_gain: float32 [1024], replicated, may hold values from 0.5 to 1.5
- query_weight: bfloat16 [1024, 512], P(None, 'branch'), may hold values from -0.1875 to 0.1875
- keyval_weight: bfloat16 [1024, 2, 128], P(None, None, 'branch'), may hold values from -0.1875 to 0.1875
- mixer_weight: bfloat16 [1024, 2, 1536], P(None, None, 'branch'), may hold values from -0.1875 to 0.1875
- state_weight: bfloat16 [1024, 2, 128], replicated, may hold values from -0.1875 to 0.1875
- step_weight: bfloat16 [1024, 24], P(None, 'branch'), may hold values from -0.1875 to 0.1875
- conv_mixer: float32 [4, 1536], P(None, 'branch'), may hold values from -3 to 3
- conv_state: float32 [4, 2, 128], replicated, may hold values from -3 to 3
- bias_mixer: float32 [1536], P('branch'), may hold values from -3 to 3
- bias_state: float32 [2, 128], replicated, may hold values from -3 to 3
- step_bias: float32 [24], P('branch'), may hold values from -6.9 to -2.3
- decay_log: float32 [24], P('branch'), may hold values from 0 to 2.77
- skip_gain: float32 [24], P('branch'), may hold values from 0.5 to 1.5
- ssd_gain: float32 [1536], P('branch'), may hold values from 0.5 to 1.5
- attn_output: bfloat16 [512, 1024], P('branch'), may hold values from -2 to 2
- ssd_output: bfloat16 [1536, 1024], P('branch'), may hold values from -0.15625 to 0.15625
- ffn_gain: float32 [1024], replicated, may hold values from 0.5 to 1.5
- gate_weight: bfloat16 [1024, 2048], replicated, may hold values from -0.1875 to 0.1875
- up_weight: bfloat16 [1024, 2048], replicated, may hold values from -0.1875 to 0.1875
- down_weight: bfloat16 [2048, 1024], replicated, may hold values from -0.125 to 0.125
- cotangent: bfloat16 [16, 1024, 1024], P('rows', 'branch'), may hold values from -6 to 6
Outputs:
- block_out: bfloat16 [16, 1024, 1024], P('rows', 'branch')
- input_grad: bfloat16 [16, 1024, 1024], P('rows', 'branch')
- norm_gain_grad: float32 [1024], replicated
- query_weight_grad: float32 [1024, 512], P('rows', 'branch')
- keyval_weight_grad: float32 [1024, 2, 128], P('rows', None, 'branch')
- mixer_weight_grad: float32 [1024, 2, 1536], P('rows', None, 'branch')
- state_weight_grad: float32 [1024, 2, 128], replicated
- step_weight_grad: float32 [1024, 24], P('rows', 'branch')
- conv_mixer_grad: float32 [4, 1536], P(None, ('branch', 'rows'))
- conv_state_grad: float32 [4, 2, 128], replicated
- bias_mixer_grad: float32 [1536], P(('branch', 'rows'))
- bias_state_grad: float32 [2, 128], replicated
- step_bias_grad: float32 [24], replicated
- decay_log_grad: float32 [24], replicated
- skip_gain_grad: float32 [24], replicated
- ssd_gain_grad: float32 [1536], P(('branch', 'rows'))
- attn_output_grad: float32 [512, 1024], P('branch', 'rows')
- ssd_output_grad: float32 [1536, 1024], P('branch', 'rows')
- ffn_gain_grad: float32 [1024], replicated
- gate_weight_grad: float32 [1024, 2048], P(None, ('branch', 'rows'))
- up_weight_grad: float32 [1024, 2048], P(None, ('branch', 'rows'))
- down_weight_grad: float32 [2048, 1024], P(('branch', 'rows'))
Inputs may be any that keep to these rules, and one draw needn't show every extreme that they name: Each row holds the 8 lengths of one pack's documents in order; they sum to 896, so the last 128 positions of every pack are padding.
All inputs are finite; a program needn't handle non-finite values.
Results may differ from a plain program's by a relative error of at most 0.017.
Values may be sent and summed in bfloat16 or wider, within the bound.
A program may use at most 192 MiB of HBM per device.

v0:
```python
import jax
import jax.numpy as jnp
from jax import lax
from jax.sharding import PartitionSpec as P

HD = 64
SH = 24
SP = 64
ABLK = 512
SBLK = 256


EPSILON = 1e-05
ROPE_BASE = 100000000000.0
PRECISE = lax.Precision.HIGHEST


def rms_scale(values):
    return lax.rsqrt(jnp.mean(values * values, axis=-1, keepdims=True) + EPSILON)


def rms_back(upstream, values, scales, gain):
    weighted = upstream * gain
    return scales * weighted - values * scales**3 * jnp.mean(
        weighted * values, axis=-1, keepdims=True
    )


def doc_tables(length_row, seq_len, doc_count):
    doc_ends = jnp.cumsum(length_row)
    starts = doc_ends - length_row
    places = jnp.arange(seq_len, dtype=jnp.int32)
    segment = jnp.sum((places[:, None] >= doc_ends[None, :]).astype(jnp.int32), axis=1)
    matches = segment[:, None] == jnp.arange(doc_count, dtype=jnp.int32)[None, :]
    offsets = jnp.sum(jnp.where(matches, starts[None, :], 0), axis=1)
    return (segment, places - offsets, (segment < doc_count).astype(jnp.float32))


def rotate(head_rows, within, direction):
    head_dim = head_rows.shape[-1]
    half_dim = head_dim // 2
    frequency = ROPE_BASE ** (-(jnp.arange(half_dim, dtype=jnp.float32) * 2.0) / head_dim)
    angles = within.astype(jnp.float32)[:, None] * frequency[None, :]
    cosine = jnp.cos(angles)[:, None, :]
    sine_part = direction * jnp.sin(angles)[:, None, :]
    first_half = head_rows[..., :half_dim]
    second_half = head_rows[..., half_dim:]
    return jnp.concatenate(
        [
            first_half * cosine - second_half * sine_part,
            second_half * cosine + first_half * sine_part,
        ],
        axis=-1,
    )


def causal_conv(conv_input, conv_weight, conv_bias, segment):
    tap_count = conv_weight.shape[0]
    result = conv_bias[None, :] + conv_weight[tap_count - 1][None, :] * conv_input
    for offset in range(1, tap_count):
        shifted = jnp.concatenate(
            [jnp.zeros((offset, conv_input.shape[1]), jnp.float32), conv_input[:-offset]], axis=0
        )
        shifted_seg = jnp.concatenate([jnp.full((offset,), -1, jnp.int32), segment[:-offset]])
        same_doc = (shifted_seg == segment).astype(jnp.float32)
        result = result + conv_weight[tap_count - 1 - offset][None, :] * shifted * same_doc[:, None]
    return result


def ssd_scan(head_inputs, step_sizes, decay_rate, state_in, state_out, segment, block_len):
    seq_len, head_count, head_dim = head_inputs.shape
    state_dim = state_in.shape[1]
    blocks = seq_len // block_len
    seg_blocks = segment.reshape(blocks, block_len)
    previous = jnp.concatenate([jnp.full((1,), -1, jnp.int32), seg_blocks[:-1, -1]])
    lower_mask = jnp.arange(block_len)[:, None] >= jnp.arange(block_len)[None, :]

    def advance(carry_state, pieces):
        input_block, step_block, in_block, out_block, seg_block, prev_seg = pieces
        log_rates = step_block * decay_rate[None, :]
        cumulative = jnp.cumsum(log_rates, axis=0)
        allowed = ((seg_block[:, None] == seg_block[None, :]) & lower_mask)[:, :, None]
        log_gaps = jnp.where(allowed, cumulative[:, None, :] - cumulative[None, :, :], 0.0)
        decays = jnp.where(allowed, jnp.exp(log_gaps), 0.0)
        intersection = jnp.dot(out_block, in_block.T, precision=PRECISE)
        weights = intersection[:, :, None] * decays * step_block[None, :, :]
        inside_part = jnp.einsum("tsh,shp->thp", weights, input_block, precision=PRECISE)
        carried = (seg_block == prev_seg).astype(jnp.float32)
        entry_decay = jnp.exp(cumulative) * carried[:, None]
        outside_part = (
            jnp.einsum("tn,hpn->thp", out_block, carry_state, precision=PRECISE)
            * entry_decay[:, :, None]
        )
        tail_mask = (seg_block == seg_block[-1]).astype(jnp.float32)
        to_end = jnp.exp(cumulative[-1][None, :] - cumulative) * tail_mask[:, None] * step_block
        kept_state = carry_state * (jnp.exp(cumulative[-1]) * carried[-1])[:, None, None]
        new_state = kept_state + jnp.einsum(
            "sh,shp,sn->hpn", to_end, input_block, in_block, precision=PRECISE
        )
        return (new_state, inside_part + outside_part)

    pieces = (
        head_inputs.reshape(blocks, block_len, head_count, head_dim),
        step_sizes.reshape(blocks, block_len, head_count),
        state_in.reshape(blocks, block_len, state_dim),
        state_out.reshape(blocks, block_len, state_dim),
        seg_blocks,
        previous,
    )
    starting = jnp.zeros((head_count, head_dim, state_dim), jnp.float32)
    final_state, outputs = lax.scan(jax.checkpoint(advance), starting, pieces)
    return outputs.reshape(seq_len, head_count, head_dim)


def mixer_local(
    mixer_proj,
    state_proj,
    step_proj,
    conv_mixer,
    conv_state,
    bias_mixer,
    bias_state,
    step_bias,
    decay_log,
    skip_gain,
    segment,
    block_len,
    head_dim,
):
    inner_dim = mixer_proj.shape[1] // 2
    state_dim = state_proj.shape[1] // 2
    gate_part = mixer_proj[:, :inner_dim]
    conv_input = jnp.concatenate([mixer_proj[:, inner_dim:], state_proj], axis=1)
    conv_weight = jnp.concatenate([conv_mixer, conv_state.reshape(conv_state.shape[0], -1)], axis=1)
    conv_bias = jnp.concatenate([bias_mixer, bias_state.reshape(-1)])
    activated = jax.nn.silu(causal_conv(conv_input, conv_weight, conv_bias, segment))
    head_count = inner_dim // head_dim
    head_inputs = activated[:, :inner_dim].reshape(-1, head_count, head_dim)
    state_in = activated[:, inner_dim : inner_dim + state_dim]
    state_out = activated[:, inner_dim + state_dim :]
    step_sizes = jax.nn.softplus(step_proj + step_bias[None, :])
    decay_rate = -jnp.exp(decay_log)
    scanned = ssd_scan(head_inputs, step_sizes, decay_rate, state_in, state_out, segment, block_len)
    combined = scanned + skip_gain[None, :, None] * head_inputs
    return combined.reshape(-1, inner_dim) * jax.nn.silu(gate_part)


def block_mask(segment, row_start, block_rows):
    places = jnp.arange(segment.shape[0], dtype=jnp.int32)
    block_seg = lax.dynamic_slice_in_dim(segment, row_start, block_rows, 0)
    block_pos = row_start + jnp.arange(block_rows, dtype=jnp.int32)
    return (block_seg[:, None] == segment[None, :]) & (block_pos[:, None] >= places[None, :])


def attend_forward(queries, key_rows, value_rows, segment, block_rows):
    scale_factor = queries.shape[-1] ** (-0.5)

    def one_block(row_start):
        block_q = lax.dynamic_slice_in_dim(queries, row_start, block_rows, 0)
        allowed = block_mask(segment, row_start, block_rows)
        raw_scores = jnp.einsum(
            "qkgd,skd->kgqs", block_q, key_rows, preferred_element_type=jnp.float32
        )
        logits = jnp.where(allowed, raw_scores * scale_factor, -jnp.inf)
        row_peak = jnp.max(logits, axis=-1, keepdims=True)
        powered = jnp.exp(logits - row_peak)
        row_total = jnp.sum(powered, axis=-1, keepdims=True)
        probs_low = (powered / row_total).astype(jnp.bfloat16)
        output = jnp.einsum(
            "kgqs,skd->qkgd", probs_low, value_rows, preferred_element_type=jnp.float32
        )
        return (output, row_peak + jnp.log(row_total))

    starts = jnp.arange(queries.shape[0] // block_rows, dtype=jnp.int32) * block_rows
    outputs, log_sums = lax.map(one_block, starts)
    return (outputs.reshape(queries.shape), log_sums)


def attend_backward(queries, key_rows, value_rows, grad_out, log_sums, segment, block_rows):
    scale_factor = queries.shape[-1] ** (-0.5)

    def one_block(carry, pieces):
        grad_keys, grad_values = carry
        row_start, block_lse = pieces
        block_q = lax.dynamic_slice_in_dim(queries, row_start, block_rows, 0)
        block_grad = lax.dynamic_slice_in_dim(grad_out, row_start, block_rows, 0)
        allowed = block_mask(segment, row_start, block_rows)
        raw_scores = jnp.einsum(
            "qkgd,skd->kgqs", block_q, key_rows, preferred_element_type=jnp.float32
        )
        logits = jnp.where(allowed, raw_scores * scale_factor, -jnp.inf)
        softmax_rows = jnp.exp(logits - block_lse)
        grad_probs = jnp.einsum(
            "qkgd,skd->kgqs", block_grad, value_rows, preferred_element_type=jnp.float32
        )
        centre = jnp.sum(softmax_rows * grad_probs, axis=-1, keepdims=True)
        grad_scores = (softmax_rows * (grad_probs - centre) * scale_factor).astype(jnp.bfloat16)
        grad_query = jnp.einsum(
            "kgqs,skd->qkgd", grad_scores, key_rows, preferred_element_type=jnp.float32
        )
        grad_keys = grad_keys + jnp.einsum(
            "kgqs,qkgd->skd", grad_scores, block_q, preferred_element_type=jnp.float32
        )
        grad_values = grad_values + jnp.einsum(
            "kgqs,qkgd->skd",
            softmax_rows.astype(jnp.bfloat16),
            block_grad,
            preferred_element_type=jnp.float32,
        )
        return ((grad_keys, grad_values), grad_query)

    starts = jnp.arange(queries.shape[0] // block_rows, dtype=jnp.int32) * block_rows
    zero_rows = jnp.zeros(key_rows.shape, jnp.float32)
    (grad_keys, grad_values), grad_queries = lax.scan(
        one_block, (zero_rows, zero_rows), (starts, log_sums)
    )
    return (grad_queries.reshape(queries.shape), grad_keys, grad_values)


def per_device(
    inputs,
    lengths,
    norm_gain,
    query_weight,
    keyval_weight,
    mixer_weight,
    state_weight,
    step_weight,
    conv_mixer,
    conv_state,
    bias_mixer,
    bias_state,
    step_bias,
    decay_log,
    skip_gain,
    ssd_gain,
    attn_output,
    ssd_output,
    ffn_gain,
    gate_weight,
    up_weight,
    down_weight,
    cotangent,
):
    branch_pos = lax.axis_index("branch")
    own_rows = inputs[0].astype(jnp.float32)
    half_len = own_rows.shape[0]
    seq_len = 2 * half_len
    model_dim = own_rows.shape[1]
    segment, within, valid_rows = doc_tables(lengths[0], seq_len, lengths.shape[1])
    own_valid = lax.dynamic_slice_in_dim(valid_rows, branch_pos * half_len, half_len, 0)
    own_scale = rms_scale(own_rows)
    own_hat = own_rows * own_scale
    normed = (own_hat * norm_gain).astype(jnp.bfloat16)
    full_normed = lax.all_gather(normed, "branch", axis=0, tiled=True)
    local_query = query_weight.shape[1] // HD
    local_keyval = keyval_weight.shape[2] // HD
    group_size = local_query // local_keyval
    keyval_flat = keyval_weight.reshape(model_dim, -1)
    mixer_flat = mixer_weight.reshape(model_dim, -1)
    state_flat = state_weight.reshape(model_dim, -1)
    query_proj = jnp.dot(full_normed, query_weight, preferred_element_type=jnp.float32)
    keyval_proj = jnp.dot(full_normed, keyval_flat, preferred_element_type=jnp.float32)
    mixer_proj = jnp.dot(full_normed, mixer_flat, preferred_element_type=jnp.float32)
    state_proj = jnp.dot(full_normed, state_flat, preferred_element_type=jnp.float32)
    step_proj = jnp.dot(full_normed, step_weight, preferred_element_type=jnp.float32)
    queries = rotate(query_proj.reshape(seq_len, local_query, HD), within, 1.0).astype(jnp.bfloat16)
    queries = queries.reshape(seq_len, local_keyval, group_size, HD)
    keyval_rows = keyval_proj.reshape(seq_len, 2, local_keyval, HD)
    key_rows = rotate(keyval_rows[:, 0], within, 1.0).astype(jnp.bfloat16)
    value_rows = keyval_rows[:, 1].astype(jnp.bfloat16)
    block_rows = min(ABLK, seq_len)
    attn_out, log_sums = attend_forward(queries, key_rows, value_rows, segment, block_rows)
    attn_low = attn_out.reshape(seq_len, -1).astype(jnp.bfloat16)

    def local_piece(
        mixer_in,
        state_in,
        step_in,
        conv_mixer_in,
        conv_state_in,
        bias_mixer_in,
        bias_state_in,
        step_bias_in,
        decay_in,
        skip_in,
    ):
        return mixer_local(
            mixer_in,
            state_in,
            step_in,
            conv_mixer_in,
            conv_state_in,
            bias_mixer_in,
            bias_state_in,
            step_bias_in,
            decay_in,
            skip_in,
            segment,
            min(SBLK, seq_len),
            SP,
        )

    gated_rows, pullback = jax.vjp(
        local_piece,
        mixer_proj,
        state_proj,
        step_proj,
        conv_mixer,
        conv_state,
        bias_mixer,
        bias_state,
        step_bias,
        decay_log,
        skip_gain,
    )
    square_sum = lax.psum(jnp.sum(gated_rows * gated_rows, axis=-1), "branch")
    gated_scale = lax.rsqrt(square_sum / (SH * SP) + EPSILON)[:, None]
    ssd_low = (gated_rows * gated_scale * ssd_gain).astype(jnp.bfloat16)
    mixer_sum = lax.psum_scatter(
        (
            jnp.dot(attn_low, attn_output, preferred_element_type=jnp.float32)
            + jnp.dot(ssd_low, ssd_output, preferred_element_type=jnp.float32)
        ).astype(jnp.bfloat16),
        "branch",
        scatter_dimension=0,
        tiled=True,
    ).astype(jnp.float32)
    hidden = own_rows + own_valid[:, None] * mixer_sum
    hidden_scale = rms_scale(hidden)
    hidden_hat = hidden * hidden_scale
    normed_ffn = (hidden_hat * ffn_gain).astype(jnp.bfloat16)
    upstream = cotangent[0]
    gate_vals = jnp.dot(normed_ffn, gate_weight, preferred_element_type=jnp.float32)
    up_vals = jnp.dot(normed_ffn, up_weight, preferred_element_type=jnp.float32)
    gate_sigmoid = jax.nn.sigmoid(gate_vals)
    act_low = (gate_vals * gate_sigmoid * up_vals).astype(jnp.bfloat16)
    ffn_out = jnp.dot(act_low, down_weight, preferred_element_type=jnp.float32)
    grad_act = jnp.einsum("rd,fd->rf", upstream, down_weight, preferred_element_type=jnp.float32)
    down_wgrad = jnp.einsum("rf,rd->fd", act_low, upstream, preferred_element_type=jnp.float32)
    grad_gate = (
        grad_act * up_vals * gate_sigmoid * (1.0 + gate_vals * (1.0 - gate_sigmoid))
    ).astype(jnp.bfloat16)
    grad_up = (grad_act * gate_vals * gate_sigmoid).astype(jnp.bfloat16)
    gate_wgrad = jnp.einsum("rd,rf->df", normed_ffn, grad_gate, preferred_element_type=jnp.float32)
    up_wgrad = jnp.einsum("rd,rf->df", normed_ffn, grad_up, preferred_element_type=jnp.float32)
    grad_normed_ffn = jnp.einsum(
        "rf,df->rd", grad_gate, gate_weight, preferred_element_type=jnp.float32
    ) + jnp.einsum("rf,df->rd", grad_up, up_weight, preferred_element_type=jnp.float32)
    ffn_grads = (
        lax.psum_scatter(gate_wgrad, ("branch", "rows"), scatter_dimension=1, tiled=True),
        lax.psum_scatter(up_wgrad, ("branch", "rows"), scatter_dimension=1, tiled=True),
        lax.psum_scatter(down_wgrad, ("branch", "rows"), scatter_dimension=0, tiled=True),
    )
    block_out = (hidden + ffn_out).astype(jnp.bfloat16)[None]
    grad_hidden = upstream.astype(jnp.float32) + rms_back(
        grad_normed_ffn, hidden, hidden_scale, ffn_gain
    )
    ffn_gain_grad = jnp.sum(grad_normed_ffn * hidden_hat, axis=0)
    grad_mixer = (own_valid[:, None] * grad_hidden).astype(jnp.bfloat16)
    full_grad_mixer = lax.all_gather(grad_mixer, "branch", axis=0, tiled=True)
    grad_attn = jnp.einsum(
        "sd,cd->sc", full_grad_mixer, attn_output, preferred_element_type=jnp.float32
    )
    grad_ssd = jnp.einsum(
        "sd,cd->sc", full_grad_mixer, ssd_output, preferred_element_type=jnp.float32
    )
    attn_out_wgrad = jnp.einsum(
        "sc,sd->cd", attn_low, full_grad_mixer, preferred_element_type=jnp.float32
    )
    ssd_out_wgrad = jnp.einsum(
        "sc,sd->cd", ssd_low, full_grad_mixer, preferred_element_type=jnp.float32
    )
    ssd_gain_wgrad = jnp.sum(grad_ssd * gated_rows * gated_scale, axis=0)
    weighted = grad_ssd * ssd_gain
    row_inner = lax.psum(jnp.sum(weighted * gated_rows, axis=-1), "branch")
    grad_gated = (
        gated_scale * weighted - gated_rows * gated_scale**3 * (row_inner / (SH * SP))[:, None]
    )
    (
        grad_mixer_proj,
        grad_state_proj,
        grad_step_proj,
        conv_mixer_wgrad,
        conv_state_wgrad,
        bias_mixer_wgrad,
        bias_state_wgrad,
        step_bias_wgrad,
        decay_log_wgrad,
        skip_gain_wgrad,
    ) = pullback(grad_gated)
    grad_attn_low = grad_attn.reshape(seq_len, local_keyval, group_size, HD).astype(jnp.bfloat16)
    grad_queries, grad_keys, grad_values = attend_backward(
        queries, key_rows, value_rows, grad_attn_low, log_sums, segment, block_rows
    )
    query_grad = (
        rotate(grad_queries.reshape(seq_len, local_query, HD), within, -1.0)
        .reshape(seq_len, -1)
        .astype(jnp.bfloat16)
    )
    keyval_grad = jnp.concatenate(
        [rotate(grad_keys, within, -1.0).reshape(seq_len, -1), grad_values.reshape(seq_len, -1)],
        axis=1,
    ).astype(jnp.bfloat16)
    mixer_grad = grad_mixer_proj.astype(jnp.bfloat16)
    step_grad = grad_step_proj.astype(jnp.bfloat16)
    partial_normed = (
        jnp.einsum("sc,dc->sd", query_grad, query_weight, preferred_element_type=jnp.float32)
        + jnp.einsum("sc,dc->sd", keyval_grad, keyval_flat, preferred_element_type=jnp.float32)
        + jnp.einsum("sc,dc->sd", mixer_grad, mixer_flat, preferred_element_type=jnp.float32)
        + jnp.einsum("sc,dc->sd", step_grad, step_weight, preferred_element_type=jnp.float32)
    )
    query_wgrad = jnp.einsum(
        "sd,sc->dc", full_normed, query_grad, preferred_element_type=jnp.float32
    )
    keyval_wgrad = jnp.einsum(
        "sd,sc->dc", full_normed, keyval_grad, preferred_element_type=jnp.float32
    ).reshape(keyval_weight.shape)
    mixer_wgrad = jnp.einsum(
        "sd,sc->dc", full_normed, mixer_grad, preferred_element_type=jnp.float32
    ).reshape(mixer_weight.shape)
    step_wgrad = jnp.einsum("sd,sc->dc", full_normed, step_grad, preferred_element_type=jnp.float32)
    own_grad_normed, own_grad_state = (
        lax.psum_scatter(
            partial_normed.astype(jnp.bfloat16), "branch", scatter_dimension=0, tiled=True
        ).astype(jnp.float32),
        lax.psum_scatter(
            grad_state_proj.astype(jnp.bfloat16), "branch", scatter_dimension=0, tiled=True
        ).astype(jnp.float32),
    )
    state_grad = own_grad_state.astype(jnp.bfloat16)
    own_grad_normed = own_grad_normed + jnp.einsum(
        "sc,dc->sd", state_grad, state_flat, preferred_element_type=jnp.float32
    )
    state_wgrad = jnp.einsum(
        "sd,sc->dc", normed, state_grad, preferred_element_type=jnp.float32
    ).reshape(state_weight.shape)
    input_grad = (grad_hidden + rms_back(own_grad_normed, own_rows, own_scale, norm_gain)).astype(
        jnp.bfloat16
    )[None]
    norm_gain_wgrad = jnp.sum(own_grad_normed * own_hat, axis=0)
    head_results = (
        lax.psum_scatter(query_wgrad, "rows", scatter_dimension=0, tiled=True),
        lax.psum_scatter(keyval_wgrad, "rows", scatter_dimension=0, tiled=True),
        lax.psum_scatter(mixer_wgrad, "rows", scatter_dimension=0, tiled=True),
        lax.psum_scatter(step_wgrad, "rows", scatter_dimension=0, tiled=True),
        lax.psum_scatter(conv_mixer_wgrad, "rows", scatter_dimension=1, tiled=True),
        lax.psum_scatter(bias_mixer_wgrad, "rows", scatter_dimension=0, tiled=True),
        lax.psum_scatter(ssd_gain_wgrad, "rows", scatter_dimension=0, tiled=True),
        lax.psum_scatter(attn_out_wgrad, "rows", scatter_dimension=1, tiled=True),
        lax.psum_scatter(ssd_out_wgrad, "rows", scatter_dimension=1, tiled=True),
    )
    local_heads = step_bias.shape[0]

    def widen(head_values):
        return lax.dynamic_update_slice_in_dim(
            jnp.zeros((SH,), jnp.float32), head_values, branch_pos * local_heads, 0
        )

    small_results = lax.psum(
        (
            norm_gain_wgrad,
            ffn_gain_grad,
            state_wgrad,
            conv_state_wgrad,
            bias_state_wgrad,
            widen(step_bias_wgrad),
            widen(decay_log_wgrad),
            widen(skip_gain_wgrad),
        ),
        ("branch", "rows"),
    )
    return (
        block_out,
        input_grad,
        small_results[0],
        head_results[0],
        head_results[1],
        head_results[2],
        small_results[2],
        head_results[3],
        head_results[4],
        small_results[3],
        head_results[5],
        small_results[4],
        small_results[5],
        small_results[6],
        small_results[7],
        head_results[6],
        head_results[7],
        head_results[8],
        small_results[1],
        ffn_grads[0],
        ffn_grads[1],
        ffn_grads[2],
    )


def solution(mesh):
    in_specs = (
        P("rows", "branch", None),
        P("rows", None),
        P(),
        P(None, "branch"),
        P(None, None, "branch"),
        P(None, None, "branch"),
        P(),
        P(None, "branch"),
        P(None, "branch"),
        P(),
        P("branch"),
        P(),
        P("branch"),
        P("branch"),
        P("branch"),
        P("branch"),
        P("branch", None),
        P("branch", None),
        P(),
        P(),
        P(),
        P(),
        P("rows", "branch", None),
    )
    out_specs = (
        P("rows", "branch", None),
        P("rows", "branch", None),
        P(),
        P("rows", "branch"),
        P("rows", None, "branch"),
        P("rows", None, "branch"),
        P(),
        P("rows", "branch"),
        P(None, ("branch", "rows")),
        P(),
        P(("branch", "rows")),
        P(),
        P(),
        P(),
        P(),
        P(("branch", "rows")),
        P("branch", "rows"),
        P("branch", "rows"),
        P(),
        P(None, ("branch", "rows")),
        P(None, ("branch", "rows")),
        P(("branch", "rows"), None),
    )
    return jax.shard_map(
        per_device, mesh=mesh, in_specs=in_specs, out_specs=out_specs, check_vma=False
    )
```

profile of v0, /device:TPU:0, one launch (start us, length us, event | category | flops | bytes accessed | tf_op | source)
XLA Modules:
  0.0 1842.5 jit_solution(6560867596815474758)
XLA Ops:
  20.2 28.3 %all-gather.3.cloned.1.call-done = bf16[1024,1024]{1,0:T(8,128)(2,1)} async-done(((bf16[512,1024]{1,0:T(8,128)(2,1)}), bf16[1024,1024]{1,0:T(8,128)(2,1)}) %all-gather.3.cloned.1.call-update) | async-done | bytes 2097168 | tf_op jit(solution)/shard_map/all_gather | solution.py:255
  90.2 141.7 %while.70 = (s32[]{:T(128)}, f32[12,64,128]{2,1,0:T(8,128)S(1)}, f32[4,256,12,64]{1,0,3,2:T(4,128)}, f32[4,12,64,128]{3,2,1,0:T(8,128)}, f32[4,256,12]{1,2,0:T(8...) while((s32[]{:T(128)}, f32[12,64,128]{2,1,0:T(8,128)S(1)}, ...), condition=%wide.region_11.12_spmd.clone, body=%wide.region_8.11_spmd.clone.sunk | while | flops 1314242560 | bytes 10585305 | solution.py:111
  103.6 17.9 dynamic_update_slice.100
  139.1 17.9 dynamic_update_slice.100
  174.5 17.9 dynamic_update_slice.100
  209.9 17.9 dynamic_update_slice.100
  255.8 24.0 %while.69 = (s32[]{:T(128)}, bf16[2,512,1,4,64]{1,4,3,2,0:T(8,128)(2,1)}, f32[2,1,4,512,1]{3,2,4,1,0:T(4,128)S(1)}, s32[2]{0:T(128)S(1)}, s32[1024]{0:T(1024)S(1...) while((s32[]{:T(128)}, ...), condition=%wide.region_7.8_spmd, body=%wide.region_4.7_spmd.sunk | while | flops 563608064 | bytes 32585960 | solution.py:175
  288.0 31.9 %reduce-scatter.16.cloned.1.call-done = bf16[512,1024]{1,0:T(8,128)(2,1)} async-done(((bf16[1024,1024]{1,0:T(8,128)(2,1)}), bf16[512,1024]{1,0:T(8,128)(2,1)}) %reduce-scatter.16.cloned.1.call-update) | async-done | bytes 1048592 | tf_op jit(solution)/shard_map/reduce_scatter | solution.py:320
  332.4 7.5 multiply_convert_fusion
  348.6 33.2 %all-gather.5.cloned.1.call-done = bf16[1024,1024]{1,0:T(8,128)(2,1)} async-done(((bf16[512,1024]{1,0:T(8,128)(2,1)}), bf16[1024,1024]{1,0:T(8,128)(2,1)}) %all-gather.5.cloned.1.call-update) | async-done | bytes 2097168 | tf_op jit(solution)/shard_map/all_gather | solution.py:361
  393.5 9.1 multiply_reduce_fusion.8
  415.7 238.1 %while.72 = (s32[]{:T(128)}, f32[12]{0:T(128)}, f32[12,64,128]{2,1,0:T(8,128)}, f32[4,256,12,64]{1,0,3,2:T(4,128)}, f32[4,256,12]{1,0,2:T(4,128)}, /*index=5*/f3...) while((s32[]{:T(128)}, f32[12]{0:T(128)}, ...), condition=%wide.region_35.36_spmd.clone, body=%wide.region_22.35_spmd.clone.sunk | while | flops 3038949376 | bytes 30968968 | solution.py:111
  448.9 17.9 dynamic_update_slice.104
  508.6 17.9 dynamic_update_slice.104
  568.2 17.9 dynamic_update_slice.104
  627.9 17.9 dynamic_update_slice.104
  685.7 63.9 %while.71 = (s32[]{:T(128)}, f32[1024,1,64]{0,2,1:T(8,128)S(1)}, f32[1024,1,64]{0,2,1:T(8,128)S(1)}, f32[2,512,1,4,64]{1,0,4,3,2:T(2,128)}, s32[2]{0:T(128)S(1)}...) while((s32[]{:T(128)}, f32[1024,1,64]{0,2,1:T(8,128)S(1)}, ...), condition=%wide.region_19.20_spmd.clone, body=%wide.region_17.19_spmd.clone.sunk | while | flops 1377565184 | bytes 120527128 | solution.py:214
  699.3 10.4 dynamic_update_slice.101
  731.3 10.4 dynamic_update_slice.101
  758.9 9.7 fusion.199
  768.6 8.4 reshape.850
  842.2 32.6 %all-reduce.24 = (f32[768]{0:T(1024)S(1)}, f32[768]{0:T(1024)S(1)}) all-reduce(f32[768]{0:T(1024)S(1)} %slice_reduce_fusion.5, f32[768]{0:T(1024)S(1)} %copy-done.128), channel_id=10, replica_groups=mesh['branch'=2,'rows'=16] {'rows'}, use_global_device_ids=true, to_apply=%region_53.54.clone | all-reduce | flops 1536 | bytes 12288
  879.6 124.4 %all-reduce.29.cloned.1.call-done = f32[1024,2,128]{2,0,1:T(8,128)} async-done(((f32[1024,2,128]{2,0,1:T(8,128)}), f32[1024,2,128]{2,0,1:T(8,128)}) %all-reduce.29.cloned.1.call-update) | async-done | bytes 1048592 | tf_op jit(solution)/shard_map/psum | solution.py:460
  1007.1 155.9 %all-reduce.31.cloned.1.call-done = (f32[1024,2,64]{2,1,0:T(2,128)}, f32[1024,2,768]{2,1,0:T(2,128)}) async-done(((f32[1024,2,64]{2,1,0:T(2,128)}, f32[1024,2,768]{2,1,0:T(2,128)}), (f32[1024,2,64]{2,1,0:T(2,128)}, f32[1024,2,768]{2,1,0:T(2,128)})) %all-reduce.31.cloned.1.call-update) | async-done | bytes 6815760
  1166.3 30.8 %reduce-scatter.18.cloned.1.call-done = bf16[512,1024]{1,0:T(8,128)(2,1)} async-done(((bf16[1024,1024]{1,0:T(8,128)(2,1)}), bf16[512,1024]{1,0:T(8,128)(2,1)}) %reduce-scatter.18.cloned.1.call-update) | async-done | bytes 1048592 | tf_op jit(solution)/shard_map/reduce_scatter | solution.py:424
  1200.5 39.6 %all-reduce.23 = (f32[1024]{0:T(1024)}, f32[4,2,128]{2,1,0:T(2,128)}, f32[2,128]{1,0:T(2,128)}, f32[24]{0:T(128)}, f32[24]{0:T(128)}, /*index=5*/f32[24]{0:T(128)}, f32[1024]{0:T(1024)}) all-reduce(f32[1024]{0:T(1024)S(1)} %get-tuple-element.1060, ...), channel_id=1, replica_groups=mesh['branch'=2,'rows'=16] {'branch','rows'}, use_global_device_ids=true, to_apply=%region_40.41 | all-reduce | flops 3400 | bytes 27200 | tf_op jit(solution)/shard_map/psum | solution.py:460
  1244.0 15.1 reduce-scatter.22.cloned.1.call-done
  1259.1 60.6 %reduce-scatter.24.cloned.1.call-done = f32[256,64]{0,1:T(8,128)} async-done(((f32[256,1024]{0,1:T(8,128)}), f32[256,64]{0,1:T(8,128)}) %reduce-scatter.24.cloned.1.call-update) | async-done | bytes 65552 | tf_op jit(solution)/shard_map/reduce_scatter | solution.py:450
  1319.7 69.9 %reduce-scatter.26.cloned.1.call-done = f32[768,64]{0,1:T(8,128)} async-done(((f32[768,1024]{0,1:T(8,128)}), f32[768,64]{0,1:T(8,128)}) %reduce-scatter.26.cloned.1.call-update) | async-done | bytes 196624 | tf_op jit(solution)/shard_map/reduce_scatter | solution.py:451
  1389.6 150.8 %reduce-scatter.28.cloned.1.call-done = f32[1024,64]{0,1:T(8,128)} async-done(((f32[1024,2048]{0,1:T(8,128)}), f32[1024,64]{0,1:T(8,128)}) %reduce-scatter.28.cloned.1.call-update) | async-done | bytes 262160 | tf_op jit(solution)/shard_map/reduce_scatter | solution.py:351
  1540.4 148.0 %reduce-scatter.30.cloned.1.call-done = f32[1024,64]{0,1:T(8,128)} async-done(((f32[1024,2048]{0,1:T(8,128)}), f32[1024,64]{0,1:T(8,128)}) %reduce-scatter.30.cloned.1.call-update) | async-done | bytes 262160 | tf_op jit(solution)/shard_map/reduce_scatter | solution.py:352
  1688.5 147.3 %reduce-scatter.32.cloned.1.call-done = f32[64,1024]{1,0:T(8,128)} async-done(((f32[2048,1024]{1,0:T(8,128)}), f32[64,1024]{1,0:T(8,128)}) %reduce-scatter.32.cloned.1.call-update) | async-done | bytes 262160 | tf_op jit(solution)/shard_map/reduce_scatter | solution.py:353
  (1024 shorter events, 547.6 us)
Async XLA Ops:
  7.2 274.5 %copy-start = (bf16[768,1024]{1,0:T(8,128)(2,1)S(1)}, bf16[768,1024]{1,0:T(8,128)(2,1)}, u32[]{:S(2)}) copy-start(bf16[768,1024]{1,0:T(8,128)(2,1)} %param.48) | copy-start | bytes 4718596
  7.2 41.3 %all-gather.3.cloned.1.call-start = ((), (), s32[]{:S(2)}) async-start(), calls=%async_computation.11 | async-start | bytes 3145728 | tf_op jit(solution)/shard_map/all_gather | solution.py:255
  12.5 307.4 %reduce-scatter.16.cloned.1.call-start = ((), (), s32[]{:S(2)}) async-start(), calls=%async_computation.12 | async-start | bytes 3145728 | tf_op jit(solution)/shard_map/reduce_scatter | solution.py:320
  12.6 239.1 %copy-start.122 = (f32[32]{0:T(128)}, f32[32]{0:T(128)S(1)}, u32[]{:S(2)}) copy-start(f32[32]{0:T(128)S(1)} %multiply_power_fusion) | copy-start | bytes 388
  17.5 376.0 %copy-start.86 = (f32[768]{0:T(1024)}, f32[768]{0:T(1024)S(1)}, u32[]{:S(2)}) copy-start(f32[768]{0:T(1024)S(1)} %mul.1156) | copy-start | bytes 9220
  18.2 233.5 %copy-start.88 = (f32[1024]{0:T(1024)}, f32[1024]{0:T(1024)S(1)}, u32[]{:S(2)}) copy-start(f32[1024]{0:T(1024)S(1)} %subtract_convert_fusion.2) | copy-start | bytes 12292
  18.8 41.9 %copy-start.100 = (f32[1024]{0:T(1024)}, f32[1024]{0:T(1024)S(1)}, u32[]{:S(2)}) copy-start(f32[1024]{0:T(1024)S(1)} %get-tuple-element.1236) | copy-start | bytes 12292
  18.8 41.9 %copy-start.102 = (f32[1024]{0:T(1024)}, f32[1024]{0:T(1024)S(1)}, u32[]{:S(2)}) copy-start(f32[1024]{0:T(1024)S(1)} %get-tuple-element.1237) | copy-start | bytes 12292
  18.8 41.9 %copy-start.104 = (f32[1024]{0:T(1024)}, f32[1024]{0:T(1024)S(1)}, u32[]{:S(2)}) copy-start(f32[1024]{0:T(1024)S(1)} %get-tuple-element.1235) | copy-start | bytes 12292
  18.9 41.9 %copy-start.92 = (f32[1,1024]{1,0:T(1,128)}, f32[1,1024]{1,0:T(1,128)S(1)}, u32[]{:S(2)}) copy-start(f32[1,1024]{1,0:T(1,128)S(1)} %get-tuple-element.1225) | copy-start | bytes 12292
  18.9 41.9 %copy-start.94 = (f32[1,1024]{1,0:T(1,128)}, f32[1,1024]{1,0:T(1,128)S(1)}, u32[]{:S(2)}) copy-start(f32[1,1024]{1,0:T(1,128)S(1)} %get-tuple-element.1226) | copy-start | bytes 12292
  18.9 41.9 %copy-start.96 = (f32[1,1024]{1,0:T(1,128)}, f32[1,1024]{1,0:T(1,128)S(1)}, u32[]{:S(2)}) copy-start(f32[1,1024]{1,0:T(1,128)S(1)} %get-tuple-element.1228) | copy-start | bytes 12292
  18.9 41.9 %copy-start.98 = (f32[1,1024]{1,0:T(1,128)}, f32[1,1024]{1,0:T(1,128)S(1)}, u32[]{:S(2)}) copy-start(f32[1,1024]{1,0:T(1,128)S(1)} %get-tuple-element.1227) | copy-start | bytes 12292
  251.7 141.7 %copy-start.114 = (f32[1024]{0:T(1024)}, f32[1024]{0:T(1024)S(1)}, u32[]{:S(2)}) copy-start(f32[1024]{0:T(1024)S(1)} %get-tuple-element.1233) | copy-start | bytes 12292
  287.9 93.8 %all-gather.5.cloned.1.call-start = ((), (), s32[]{:S(2)}) async-start(), calls=%async_computation.13 | async-start | bytes 3145728 | tf_op jit(solution)/shard_map/all_gather | solution.py:361
  288.0 57.8 %copy-start.106 = (f32[512]{0:T(512)}, f32[512]{0:T(512)S(1)}, u32[]{:S(2)}) copy-start(f32[512]{0:T(512)S(1)} %dynamic_slice.143) | copy-start | bytes 6148
  348.5 428.6 %reduce-scatter.20.cloned.1.call-start = ((), (), s32[]{:S(2)}) async-start(), calls=%async_computation.15 | async-start | bytes 786432 | tf_op jit(solution)/shard_map/reduce_scatter | solution.py:427
  683.1 193.7 %reduce-scatter.36.cloned.1.call-start = ((), (), s32[]{:S(2)}) async-start(), calls=%async_computation.24 | async-start | bytes 417792
  755.1 123.1 %reduce-scatter.34.cloned.1.call-start = ((), (), s32[]{:S(2)}) async-start(), calls=%async_computation.23 | async-start | bytes 557056
  777.0 227.1 %all-reduce.29.cloned.1.call-start = ((), (), s32[]{:S(2)}) async-start(), calls=%async_computation.17 | async-start | bytes 2097152 | tf_op jit(solution)/shard_map/psum | solution.py:460
  779.9 383.2 %all-reduce.31.cloned.1.call-start = ((), (), s32[]{:S(2)}) async-start(), calls=%async_computation.25 | async-start | bytes 14680064
  783.3 413.8 %reduce-scatter.18.cloned.1.call-start = ((), (), s32[]{:S(2)}) async-start(), calls=%async_computation.14 | async-start | bytes 3145728 | tf_op jit(solution)/shard_map/reduce_scatter | solution.py:424
  795.6 463.5 %reduce-scatter.22.cloned.1.call-start = ((), (), s32[]{:S(2)}) async-start(), calls=%async_computation.16 | async-start | bytes 1114112 | tf_op jit(solution)/shard_map/reduce_scatter | solution.py:443
  799.0 520.7 %reduce-scatter.24.cloned.1.call-start = ((), (), s32[]{:S(2)}) async-start(), calls=%async_computation.18 | async-start | bytes 1114112 | tf_op jit(solution)/shard_map/reduce_scatter | solution.py:450
  802.6 587.0 %reduce-scatter.26.cloned.1.call-start = ((), (), s32[]{:S(2)}) async-start(), calls=%async_computation.19 | async-start | bytes 3342336 | tf_op jit(solution)/shard_map/reduce_scatter | solution.py:451
  808.9 731.6 %reduce-scatter.28.cloned.1.call-start = ((), (), s32[]{:S(2)}) async-start(), calls=%async_computation.20 | async-start | bytes 8650752 | tf_op jit(solution)/shard_map/reduce_scatter | solution.py:351
  817.4 871.1 %reduce-scatter.30.cloned.1.call-start = ((), (), s32[]{:S(2)}) async-start(), calls=%async_computation.21 | async-start | bytes 8650752 | tf_op jit(solution)/shard_map/reduce_scatter | solution.py:352
  824.9 1010.8 %reduce-scatter.32.cloned.1.call-start = ((), (), s32[]{:S(2)}) async-start(), calls=%async_computation.22 | async-start | bytes 8650752 | tf_op jit(solution)/shard_map/reduce_scatter | solution.py:353
  842.2 354.9 %copy-start.73 = (bf16[512,256]{1,0:T(8,128)(2,1)S(1)}, bf16[512,256]{1,0:T(8,128)(2,1)}, u32[]{:S(2)}) copy-start(bf16[512,256]{1,0:T(8,128)(2,1)} %reduce-scatter.20.cloned.1.call-done) | copy-start | bytes 786436
  842.2 354.9 %copy-start.139 = (bf16[1024,2,128]{2,1,0:T(2,128)(2,1)S(1)}, bf16[1024,2,128]{2,1,0:T(2,128)(2,1)}, u32[]{:S(2)}) copy-start(bf16[1024,2,128]{2,1,0:T(2,128)(2,1)} %param.37) | copy-start | bytes 1572868
  1164.5 75.5 %copy-start.121 = (f32[512]{0:T(512)S(1)}, f32[512]{0:T(512)}, u32[]{:S(2)}) copy-start(f32[512]{0:T(512)} %get-tuple-element.1238) | copy-start | bytes 6148
  1240.0 595.7 %copy-start.1 = (bf16[768,1024]{1,0:T(8,128)(2,1)S(1)}, bf16[768,1024]{1,0:T(8,128)(2,1)}, u32[]{:S(2)}) copy-start(bf16[768,1024]{1,0:T(8,128)(2,1)} %param.48) | copy-start | bytes 4718596
  (219 other events, 2157.4 us)
Sparse Core Ops, SparseCore 0:
  12.6 35.8 all-gather.2
  288.0 31.8 reduce-scatter.15
  348.6 33.1 all-gather.4
  683.1 14.5 reduce-scatter.19
  755.3 55.5 reduce-scatter.35
  814.7 54.8 reduce-scatter.33
  875.3 128.7 all-reduce.28
  1009.0 154.0 all-reduce.30
  1165.3 31.7 reduce-scatter.17
  1201.6 57.4 reduce-scatter.21
  1263.3 56.3 reduce-scatter.23
  1324.4 65.1 reduce-scatter.25
  1392.6 147.8 reduce-scatter.27
  1543.3 145.1 reduce-scatter.29
  1691.3 144.4 reduce-scatter.31
where the time goes:
time: 1860 us; the launch traced here: 1840 us
  waiting for transfers between devices  997 us (54%)
  local copies, waits for them, and re-layouts  337 us (18%)
  matrix products  265 us (14%)
  other arithmetic  132 us (7%)
  blocking collectives  82.1 us (4%)
    unnamed x18, waiting for transfers between devices  156 us
    dynamic_update_slice x24, local copies, waits for them, and re-layouts, ssd_scan(): final_state, outputs = lax.scan(jax.checkpoint(advance), starting, pieces)  155 us
    reduce_scatter x1, waiting for transfers between devices, per_device(): lax.psum_scatter(gate_wgrad, ('branch', 'rows'), scatter_dimension=1, til...  151 us
    reduce_scatter x1, waiting for transfers between devices, per_device(): lax.psum_scatter(up_wgrad, ('branch', 'rows'), scatter_dimension=1, tiled...  148 us
    reduce_scatter x1, waiting for transfers between devices, per_device(): lax.psum_scatter(down_wgrad, ('branch', 'rows'), scatter_dimension=0, til...  147 us
    psum x1, waiting for transfers between devices, per_device(): lax.psum((norm_gain_wgrad, ffn_gain_grad, state_wgrad, conv_state_wgrad,...  124 us
    reduce_scatter x1, waiting for transfers between devices, per_device(): lax.psum_scatter(ssd_out_wgrad, 'rows', scatter_dimension=1, tiled=True)  69.9 us
    reduce_scatter x1, waiting for transfers between devices, per_device(): lax.psum_scatter(attn_out_wgrad, 'rows', scatter_dimension=1, tiled=True)  60.6 us
  transfers between devices with their start and end apart: 15, of which 12 were waited for; matrix products, arithmetic and copies ran while one was open for 9% of the time, Pallas kernels for 0%

commit v1 on v0

--- a/solution.py
+++ b/solution.py
@@ -27,7 +27,8 @@
 
 
 def doc_tables(length_row, seq_len, doc_count):
-    doc_ends = jnp.cumsum(length_row)
+    order = jnp.arange(doc_count, dtype=jnp.int32)
+    doc_ends = jnp.sum(jnp.where(order[:, None] >= order[None, :], length_row[None, :], 0), axis=1)
     starts = doc_ends - length_row
     places = jnp.arange(seq_len, dtype=jnp.int32)
     segment = jnp.sum((places[:, None] >= doc_ends[None, :]).astype(jnp.int32), axis=1)
@@ -78,7 +79,7 @@
     def advance(carry_state, pieces):
         input_block, step_block, in_block, out_block, seg_block, prev_seg = pieces
         log_rates = step_block * decay_rate[None, :]
-        cumulative = jnp.cumsum(log_rates, axis=0)
+        cumulative = jnp.dot(lower_mask.astype(jnp.float32), log_rates, precision=PRECISE)
         allowed = ((seg_block[:, None] == seg_block[None, :]) & lower_mask)[:, :, None]
         log_gaps = jnp.where(allowed, cumulative[:, None, :] - cumulative[None, :, :], 0.0)
         decays = jnp.where(allowed, jnp.exp(log_gaps), 0.0)
@@ -217,6 +218,73 @@
     return (grad_queries.reshape(queries.shape), grad_keys, grad_values)
 
 
+def bits_of(count):
+    return count.bit_length() - 1
+
+
+def swap_halves(values, axis_name, bit, size):
+    pairs = [(item, item ^ (1 << bit)) for item in range(size)]
+    return lax.ppermute(values, axis_name, pairs)
+
+
+def halve(values, place, my_bit, axis_name, bit, size):
+    owners = values.shape[0]
+    high = 1 << place
+    parts = values.reshape((high, 2, owners // (2 * high)) + values.shape[1:])
+    sent = lax.dynamic_index_in_dim(parts, 1 - my_bit, 1, keepdims=False)
+    kept = lax.dynamic_index_in_dim(parts, my_bit, 1, keepdims=False)
+    got = swap_halves(sent, axis_name, bit, size)
+    total = (kept.astype(jnp.float32) + got.astype(jnp.float32)).astype(values.dtype)
+    return total.reshape((owners // 2,) + values.shape[1:])
+
+
+def scatter_sum(values, digits, order):
+    left = list(digits)
+    for digit in order:
+        axis_name, bit, size = digit
+        my_bit = (lax.axis_index(axis_name) >> bit) & 1
+        values = halve(values, left.index(digit), my_bit, axis_name, bit, size)
+        left.remove(digit)
+    return values[0]
+
+
+def gather_all(values, digits, order):
+    values = values[None]
+    left = []
+    for digit in order:
+        axis_name, bit, size = digit
+        my_bit = (lax.axis_index(axis_name) >> bit) & 1
+        got = swap_halves(values, axis_name, bit, size)
+        place = sum(1 for item in left if digits.index(item) < digits.index(digit))
+        high = 1 << place
+        owners = values.shape[0]
+        mine = values.reshape((high, 1, owners // high) + values.shape[1:])
+        other = got.reshape(mine.shape)
+        first = jnp.where(my_bit == 0, mine, other)
+        second = jnp.where(my_bit == 0, other, mine)
+        values = jnp.concatenate([first, second], axis=1).reshape((owners * 2,) + values.shape[1:])
+        left.append(digit)
+    return values
+
+
+def other_branch(values):
+    return lax.ppermute(values, "branch", [(0, 1), (1, 0)])
+
+
+def both_halves(values, branch_pos):
+    got = other_branch(values)
+    return jnp.concatenate(
+        [jnp.where(branch_pos == 0, values, got), jnp.where(branch_pos == 0, got, values)], axis=0
+    )
+
+
+def own_half_sum(values, branch_pos):
+    half = values.shape[0] // 2
+    sent = lax.dynamic_slice_in_dim(values, (1 - branch_pos) * half, half, 0)
+    kept = lax.dynamic_slice_in_dim(values, branch_pos * half, half, 0)
+    return kept.astype(jnp.float32) + other_branch(sent).astype(jnp.float32)
+
+
 def per_device(
     inputs,
     lengths,
@@ -243,6 +311,12 @@
     cotangent,
 ):
     branch_pos = lax.axis_index("branch")
+    row_count = lax.axis_size("rows")
+    row_bits = bits_of(row_count)
+    row_digits = [("rows", bit, row_count) for bit in range(row_bits - 1, -1, -1)]
+    all_digits = [("branch", 0, 2)] + row_digits
+    upward = row_digits[::-1]
+    full_order = [upward[0]] + [all_digits[0]] + upward[1:]
     own_rows = inputs[0].astype(jnp.float32)
     half_len = own_rows.shape[0]
     seq_len = 2 * half_len
@@ -252,7 +326,7 @@
     own_scale = rms_scale(own_rows)
     own_hat = own_rows * own_scale
     normed = (own_hat * norm_gain).astype(jnp.bfloat16)
-    full_normed = lax.all_gather(normed, "branch", axis=0, tiled=True)
+    full_normed = both_halves(normed, branch_pos)
     local_query = query_weight.shape[1] // HD
     local_keyval = keyval_weight.shape[2] // HD
     group_size = local_query // local_keyval
@@ -317,15 +391,13 @@
     square_sum = lax.psum(jnp.sum(gated_rows * gated_rows, axis=-1), "branch")
     gated_scale = lax.rsqrt(square_sum / (SH * SP) + EPSILON)[:, None]
     ssd_low = (gated_rows * gated_scale * ssd_gain).astype(jnp.bfloat16)
-    mixer_sum = lax.psum_scatter(
+    mixer_sum = own_half_sum(
         (
             jnp.dot(attn_low, attn_output, preferred_element_type=jnp.float32)
             + jnp.dot(ssd_low, ssd_output, preferred_element_type=jnp.float32)
         ).astype(jnp.bfloat16),
-        "branch",
-        scatter_dimension=0,
-        tiled=True,
-    ).astype(jnp.float32)
+        branch_pos,
+    )
     hidden = own_rows + own_valid[:, None] * mixer_sum
     hidden_scale = rms_scale(hidden)
     hidden_hat = hidden * hidden_scale
@@ -337,20 +409,28 @@
     act_low = (gate_vals * gate_sigmoid * up_vals).astype(jnp.bfloat16)
     ffn_out = jnp.dot(act_low, down_weight, preferred_element_type=jnp.float32)
     grad_act = jnp.einsum("rd,fd->rf", upstream, down_weight, preferred_element_type=jnp.float32)
-    down_wgrad = jnp.einsum("rf,rd->fd", act_low, upstream, preferred_element_type=jnp.float32)
+    down_wgrad = jnp.einsum("rf,rd->fd", act_low, upstream, preferred_element_type=jnp.float32).astype(jnp.bfloat16)
     grad_gate = (
         grad_act * up_vals * gate_sigmoid * (1.0 + gate_vals * (1.0 - gate_sigmoid))
     ).astype(jnp.bfloat16)
     grad_up = (grad_act * gate_vals * gate_sigmoid).astype(jnp.bfloat16)
-    gate_wgrad = jnp.einsum("rd,rf->df", normed_ffn, grad_gate, preferred_element_type=jnp.float32)
-    up_wgrad = jnp.einsum("rd,rf->df", normed_ffn, grad_up, preferred_element_type=jnp.float32)
+    gate_wgrad = jnp.einsum("rf,rd->fd", grad_gate, normed_ffn, preferred_element_type=jnp.float32).astype(jnp.bfloat16)
+    up_wgrad = jnp.einsum("rf,rd->fd", grad_up, normed_ffn, preferred_element_type=jnp.float32).astype(jnp.bfloat16)
     grad_normed_ffn = jnp.einsum(
         "rf,df->rd", grad_gate, gate_weight, preferred_element_type=jnp.float32
     ) + jnp.einsum("rf,df->rd", grad_up, up_weight, preferred_element_type=jnp.float32)
+
+    def owner_rows(partial):
+        return partial.reshape((2 * row_count, -1) + partial.shape[1:])
+
+    ffn_sums = [
+        scatter_sum(owner_rows(item), all_digits, full_order)
+        for item in (gate_wgrad, up_wgrad, down_wgrad)
+    ]
     ffn_grads = (
-        lax.psum_scatter(gate_wgrad, ("branch", "rows"), scatter_dimension=1, tiled=True),
-        lax.psum_scatter(up_wgrad, ("branch", "rows"), scatter_dimension=1, tiled=True),
-        lax.psum_scatter(down_wgrad, ("branch", "rows"), scatter_dimension=0, tiled=True),
+        ffn_sums[0].astype(jnp.float32).T,
+        ffn_sums[1].astype(jnp.float32).T,
+        ffn_sums[2].astype(jnp.float32),
     )
     block_out = (hidden + ffn_out).astype(jnp.bfloat16)[None]
     grad_hidden = upstream.astype(jnp.float32) + rms_back(
@@ -358,7 +438,7 @@
     )
     ffn_gain_grad = jnp.sum(grad_normed_ffn * hidden_hat, axis=0)
     grad_mixer = (own_valid[:, None] * grad_hidden).astype(jnp.bfloat16)
-    full_grad_mixer = lax.all_gather(grad_mixer, "branch", axis=0, tiled=True)
+    full_grad_mixer = both_halves(grad_mixer, branch_pos)
     grad_attn = jnp.einsum(
         "sd,cd->sc", full_grad_mixer, attn_output, preferred_element_type=jnp.float32
     )
@@ -366,11 +446,11 @@
         "sd,cd->sc", full_grad_mixer, ssd_output, preferred_element_type=jnp.float32
     )
     attn_out_wgrad = jnp.einsum(
-        "sc,sd->cd", attn_low, full_grad_mixer, preferred_element_type=jnp.float32
-    )
+        "sd,sc->dc", full_grad_mixer, attn_low, preferred_element_type=jnp.float32
+    ).astype(jnp.bfloat16)
     ssd_out_wgrad = jnp.einsum(
-        "sc,sd->cd", ssd_low, full_grad_mixer, preferred_element_type=jnp.float32
-    )
+        "sd,sc->dc", full_grad_mixer, ssd_low, preferred_element_type=jnp.float32
+    ).astype(jnp.bfloat16)
     ssd_gain_wgrad = jnp.sum(grad_ssd * gated_rows * gated_scale, axis=0)
     weighted = grad_ssd * ssd_gain
     row_inner = lax.psum(jnp.sum(weighted * gated_rows, axis=-1), "branch")
@@ -420,55 +500,95 @@
         "sd,sc->dc", full_normed, mixer_grad, preferred_element_type=jnp.float32
     ).reshape(mixer_weight.shape)
     step_wgrad = jnp.einsum("sd,sc->dc", full_normed, step_grad, preferred_element_type=jnp.float32)
-    own_grad_normed, own_grad_state = (
-        lax.psum_scatter(
-            partial_normed.astype(jnp.bfloat16), "branch", scatter_dimension=0, tiled=True
-        ).astype(jnp.float32),
-        lax.psum_scatter(
-            grad_state_proj.astype(jnp.bfloat16), "branch", scatter_dimension=0, tiled=True
-        ).astype(jnp.float32),
-    )
-    state_grad = own_grad_state.astype(jnp.bfloat16)
-    own_grad_normed = own_grad_normed + jnp.einsum(
-        "sc,dc->sd", state_grad, state_flat, preferred_element_type=jnp.float32
-    )
+    state_low = grad_state_proj.astype(jnp.bfloat16)
+    partial_normed = partial_normed + jnp.einsum(
+        "sc,dc->sd", state_low, state_flat, preferred_element_type=jnp.float32
+    )
+    own_grad_normed = own_half_sum(partial_normed.astype(jnp.bfloat16), branch_pos)
     state_wgrad = jnp.einsum(
-        "sd,sc->dc", normed, state_grad, preferred_element_type=jnp.float32
-    ).reshape(state_weight.shape)
+        "sd,sc->dc", full_normed, state_low, preferred_element_type=jnp.float32
+    )
     input_grad = (grad_hidden + rms_back(own_grad_normed, own_rows, own_scale, norm_gain)).astype(
         jnp.bfloat16
     )[None]
     norm_gain_wgrad = jnp.sum(own_grad_normed * own_hat, axis=0)
+    def row_sum(partial):
+        low = partial.astype(jnp.bfloat16)
+        return scatter_sum(
+            low.reshape((row_count, -1) + low.shape[1:]), row_digits, upward
+        ).astype(jnp.float32)
+
+    query_sum = row_sum(query_wgrad)
+    keyval_sum = row_sum(keyval_wgrad.reshape(model_dim, -1))
+    mixer_wsum = row_sum(mixer_wgrad.reshape(model_dim, -1))
+    step_sum = row_sum(step_wgrad)
+    attn_out_sum = row_sum(attn_out_wgrad).T
+    ssd_out_sum = row_sum(ssd_out_wgrad).T
+    state_part = scatter_sum(
+        owner_rows(state_wgrad.astype(jnp.bfloat16)), all_digits, full_order
+    )
+    state_sum = gather_all(state_part, all_digits, full_order[::-1]).astype(jnp.float32)
+    local_heads = step_bias.shape[0]
+    local_inner = bias_mixer.shape[0]
+
+    def widen(head_values):
+        full = jnp.zeros(head_values.shape[:-1] + (2 * head_values.shape[-1],), jnp.float32)
+        return lax.dynamic_update_slice_in_dim(
+            full, head_values, branch_pos * head_values.shape[-1], head_values.ndim - 1
+        )
+
+    small = [
+        norm_gain_wgrad,
+        ffn_gain_grad,
+        conv_state_wgrad,
+        bias_state_wgrad,
+        widen(step_bias_wgrad),
+        widen(decay_log_wgrad),
+        widen(skip_gain_wgrad),
+        widen(conv_mixer_wgrad),
+        widen(bias_mixer_wgrad),
+        widen(ssd_gain_wgrad),
+    ]
+    sizes = [item.size for item in small]
+    flat = jnp.concatenate([item.reshape(-1) for item in small])
+    unit = 2 * row_count * 128
+    padded = -(-flat.shape[0] // unit) * unit
+    flat = jnp.pad(flat, (0, padded - flat.shape[0]))
+    flat_part = scatter_sum(flat.reshape(2 * row_count, -1, 128), all_digits, full_order)
+    flat_sum = gather_all(flat_part, all_digits, full_order[::-1]).reshape(-1)
+    sums = []
+    begin = 0
+    for item, size in zip(small, sizes):
+        sums.append(flat_sum[begin : begin + size].reshape(item.shape))
+        begin += size
+    row_pos = lax.axis_index("rows")
+
+    def own_columns(total):
+        width = local_inner // row_count
+        return lax.dynamic_slice_in_dim(
+            total, branch_pos * local_inner + row_pos * width, width, total.ndim - 1
+        )
+
+    small_results = (
+        sums[0],
+        sums[1],
+        state_sum.reshape(state_weight.shape),
+        sums[2],
+        sums[3],
+        sums[4],
+        sums[5],
+        sums[6],
+    )
     head_results = (
-        lax.psum_scatter(query_wgrad, "rows", scatter_dimension=0, tiled=True),
-        lax.psum_scatter(keyval_wgrad, "rows", scatter_dimension=0, tiled=True),
-        lax.psum_scatter(mixer_wgrad, "rows", scatter_dimension=0, tiled=True),
-        lax.psum_scatter(step_wgrad, "rows", scatter_dimension=0, tiled=True),
-        lax.psum_scatter(conv_mixer_wgrad, "rows", scatter_dimension=1, tiled=True),
-        lax.psum_scatter(bias_mixer_wgrad, "rows", scatter_dimension=0, tiled=True),
-        lax.psum_scatter(ssd_gain_wgrad, "rows", scatter_dimension=0, tiled=True),
-        lax.psum_scatter(attn_out_wgrad, "rows", scatter_dimension=1, tiled=True),
-        lax.psum_scatter(ssd_out_wgrad, "rows", scatter_dimension=1, tiled=True),
-    )
-    local_heads = step_bias.shape[0]
-
-    def widen(head_values):
-        return lax.dynamic_update_slice_in_dim(
-            jnp.zeros((SH,), jnp.float32), head_values, branch_pos * local_heads, 0
-        )
-
-    small_results = lax.psum(
-        (
-            norm_gain_wgrad,
-            ffn_gain_grad,
-            state_wgrad,
-            conv_state_wgrad,
-            bias_state_wgrad,
-            widen(step_bias_wgrad),
-            widen(decay_log_wgrad),
-            widen(skip_gain_wgrad),
-        ),
-        ("branch", "rows"),
+        query_sum,
+        keyval_sum.reshape((-1,) + keyval_weight.shape[1:]),
+        mixer_wsum.reshape((-1,) + mixer_weight.shape[1:]),
+        step_sum,
+        own_columns(sums[7]),
+        own_columns(sums[8]),
+        own_columns(sums[9]),
+        attn_out_sum,
+        ssd_out_sum,
     )
     return (
         block_out,

time: 1860 us -> 1050 us (0.56)
  waiting for transfers between devices: 997 us -> 227 us
  blocking collectives: 82.1 us -> 9.99 us
  starting transfers between devices: 1.41 us -> 68.1 us
  matrix products: 265 us -> 233 us
    reduce_scatter x9 -> x0, waiting for transfers between devices: 654 us -> none  [the longest x1 151 us: per_device(): lax.psum_scatter(gate_wgrad, ('branch', 'rows'), scatter_dimension=1, til...]
    ppermute x0 -> x63, waiting for transfers between devices: none -> 227 us  [the longest x59 180 us: swap_halves(): return lax.ppermute(values, axis_name, pairs)]
    unnamed x18 -> x0, waiting for transfers between devices: 156 us -> none
    psum x1 -> x0, waiting for transfers between devices: 124 us -> none  [per_device(): lax.psum((norm_gain_wgrad, ffn_gain_grad, state_wgrad, conv_state_wgrad,...]
    ppermute x0 -> x63, starting transfers between devices: none -> 68.1 us  [the longest x59 60.5 us: swap_halves(): return lax.ppermute(values, axis_name, pairs)]
    all_gather x2 -> x0, waiting for transfers between devices: 61.5 us -> none  [the longest x1 33.2 us: per_device(): full_grad_mixer = lax.all_gather(grad_mixer, 'branch', axis=0, tiled=True)]
    psum x1 -> x0, blocking collectives: 39.6 us -> none  [per_device(): lax.psum((norm_gain_wgrad, ffn_gain_grad, state_wgrad, conv_state_wgrad,...]
    unnamed x1 -> x0, blocking collectives: 32.6 us -> none
  transfers between devices with their start and end apart: 15 -> 63, of which waited for: 12 -> 43; matrix products, arithmetic and copies ran while one was open for 9% -> 43% of each run, Pallas kernels for 0% -> 0%
where the time goes in v1:
time: 1050 us; the launch traced here: 1040 us
  local copies, waits for them, and re-layouts  347 us (33%)
  matrix products  233 us (22%)
  waiting for transfers between devices  227 us (22%)
  other arithmetic  138 us (13%)
  starting transfers between devices  68.1 us (6%)
  loops' own time  11.2 us (1%)
    ppermute x59, waiting for transfers between devices, swap_halves(): return lax.ppermute(values, axis_name, pairs)  180 us
    dynamic_update_slice x24, local copies, waits for them, and re-layouts, ssd_scan(): final_state, outputs = lax.scan(jax.checkpoint(advance), starting, pieces)  155 us
    ppermute x59, starting transfers between devices, swap_halves(): return lax.ppermute(values, axis_name, pairs)  60.5 us
    dot_general x12, matrix products, advance(): jnp.einsum('tsh,shp->thp', weights, input_block, precision=PRECISE)  51.8 us
    ppermute x4, waiting for transfers between devices, other_branch(): return lax.ppermute(values, 'branch', [(0, 1), (1, 0)])  47 us
    unnamed x320, local copies, waits for them, and re-layouts  38.6 us
    dynamic_slice x20, local copies, waits for them, and re-layouts, ssd_scan(): final_state, outputs = lax.scan(jax.checkpoint(advance), starting, pieces)  23.8 us
    dynamic_update_slice x4, local copies, waits for them, and re-layouts, attend_forward(): outputs, log_sums = lax.map(one_block, starts)  21.9 us
  transfers between devices with their start and end apart: 63, of which 43 were waited for; matrix products, arithmetic and copies ran while one was open for 43% of the time, Pallas kernels for 0%

profile of v1, /device:TPU:0, one launch (start us, length us, event | category | flops | bytes accessed | tf_op | source)
XLA Modules:
  0.0 1037.9 jit_solution(5288879875677724946)
XLA Ops:
  17.0 14.8 %collective-permute-done = bf16[512,1024]{1,0:T(8,128)(2,1)} collective-permute-done((bf16[512,1024]{1,0:T(8,128)(2,1)}, bf16[512,1024]{1,0:T(8,128)(2,1)}, u32[]{:S(2)}, u32[]{:S(2)}) %collective-permute-start) | collective-permute-done | bytes 1048608 | tf_op jit(solution)/shard_map/ppermute | solution.py:271
  44.4 5.5 fusion.178
  71.5 143.0 %while.70 = (s32[]{:T(128)}, f32[12,64,128]{2,1,0:T(8,128)S(1)}, f32[4,256,12,64]{1,0,3,2:T(4,128)}, f32[4,12,64,128]{3,2,1,0:T(8,128)}, f32[4,256,12]{1,2,0:T(8...) while((s32[]{:T(128)}, f32[12,64,128]{2,1,0:T(8,128)S(1)}, ...), condition=%wide.region_9.10_spmd.clone, body=%wide.region_8.9_spmd.clone.sunk | while | flops 1323417600 | bytes 10412977 | solution.py:112
  85.3 17.9 %dynamic_update_slice.114 = f32[4,256,12,64]{1,0,3,2:T(4,128)} dynamic-update-slice(f32[4,256,12,64]{1,0,3,2:T(4,128)} %get-tuple-element.1559, f32[1,256,12,64]{1,0,3,2:T(1,128)S(1)} %copy.371, s32[]{:T(128)} %get-tuple-element.1557, s32[]{:T(128)} %constant.456.clone.1..sunk.1, s32[]{:T(128)} %constant.456.clone.1..sunk.1, s32[]{:T(128)} %constant.456.clone.1..sunk.1) | dynamic-update-slice | bytes 1572868 | tf_op jit(solution)/shard_map/jvp()/while/body/jit(dynamic_update_index_in_dim)/dynamic_update_slice | solution.py:112
  121.0 17.9 %dynamic_update_slice.114 = f32[4,256,12,64]{1,0,3,2:T(4,128)} dynamic-update-slice(f32[4,256,12,64]{1,0,3,2:T(4,128)} %get-tuple-element.1559, f32[1,256,12,64]{1,0,3,2:T(1,128)S(1)} %copy.371, s32[]{:T(128)} %get-tuple-element.1557, s32[]{:T(128)} %constant.456.clone.1..sunk.1, s32[]{:T(128)} %constant.456.clone.1..sunk.1, s32[]{:T(128)} %constant.456.clone.1..sunk.1) | dynamic-update-slice | bytes 1572868 | tf_op jit(solution)/shard_map/jvp()/while/body/jit(dynamic_update_index_in_dim)/dynamic_update_slice | solution.py:112
  156.8 17.9 %dynamic_update_slice.114 = f32[4,256,12,64]{1,0,3,2:T(4,128)} dynamic-update-slice(f32[4,256,12,64]{1,0,3,2:T(4,128)} %get-tuple-element.1559, f32[1,256,12,64]{1,0,3,2:T(1,128)S(1)} %copy.371, s32[]{:T(128)} %get-tuple-element.1557, s32[]{:T(128)} %constant.456.clone.1..sunk.1, s32[]{:T(128)} %constant.456.clone.1..sunk.1, s32[]{:T(128)} %constant.456.clone.1..sunk.1) | dynamic-update-slice | bytes 1572868 | tf_op jit(solution)/shard_map/jvp()/while/body/jit(dynamic_update_index_in_dim)/dynamic_update_slice | solution.py:112
  192.6 17.9 %dynamic_update_slice.114 = f32[4,256,12,64]{1,0,3,2:T(4,128)} dynamic-update-slice(f32[4,256,12,64]{1,0,3,2:T(4,128)} %get-tuple-element.1559, f32[1,256,12,64]{1,0,3,2:T(1,128)S(1)} %copy.371, s32[]{:T(128)} %get-tuple-element.1557, s32[]{:T(128)} %constant.456.clone.1..sunk.1, s32[]{:T(128)} %constant.456.clone.1..sunk.1, s32[]{:T(128)} %constant.456.clone.1..sunk.1) | dynamic-update-slice | bytes 1572868 | tf_op jit(solution)/shard_map/jvp()/while/body/jit(dynamic_update_index_in_dim)/dynamic_update_slice | solution.py:112
  222.7 6.6 multiply_reduce_fusion.11
  238.0 24.4 %while.69 = (s32[]{:T(128)}, bf16[2,512,1,4,64]{1,4,3,2,0:T(8,128)(2,1)}, f32[2,1,4,512,1]{3,2,4,1,0:T(4,128)S(1)}, s32[2]{0:T(128)S(1)}, s32[1024]{0:T(1024)S(1...) while((s32[]{:T(128)}, ...), condition=%wide.region_7.8_spmd, body=%wide.region_4.7_spmd.sunk | while | flops 563608064 | bytes 32585960 | solution.py:176
  278.3 16.6 %collective-permute-done.1 = bf16[512,1024]{1,0:T(8,128)(2,1)} collective-permute-done((bf16[512,1024]{1,0:T(8,128)(2,1)}, bf16[512,1024]{1,0:T(8,128)(2,1)}, u32[]{:S(2)}, u32[]{:S(2)}) %collective-permute-start.1) | collective-permute-done | bytes 1048608 | tf_op jit(solution)/shard_map/ppermute | solution.py:271
  307.8 5.5 fusion.322
  335.7 15.5 %collective-permute-done.2 = bf16[512,1024]{1,0:T(8,128)(2,1)S(1)} collective-permute-done((bf16[512,1024]{1,0:T(8,128)(2,1)S(1)}, bf16[512,1024]{1,0:T(8,128)(2,1)S(1)}, u32[]{:S(2)}, u32[]{:S(2)}) %collective-permute-start.2) | collective-permute-done | bytes 1048608 | tf_op jit(solution)/shard_map/ppermute | solution.py:271
  367.7 9.1 multiply_reduce_fusion.9
  380.4 5.2 reshape.1434
  390.2 219.6 %while.72 = (s32[]{:T(128)}, f32[12]{0:T(128)}, f32[12,64,128]{2,1,0:T(8,128)S(1)}, f32[4,256,12,64]{1,0,3,2:T(4,128)}, f32[4,256,12]{1,0,2:T(4,128)}, /*index=5...) while((s32[]{:T(128)}, f32[12]{0:T(128)}, ...), condition=%wide.region_28.29_spmd.clone, body=%wide.region_19.28_spmd.clone.sunk | while | flops 3057037312 | bytes 26190060 | solution.py:112
  423.1 17.9 %dynamic_update_slice.118 = f32[4,256,12,64]{1,0,3,2:T(4,128)} dynamic-update-slice(f32[4,256,12,64]{1,0,3,2:T(4,128)} %get-tuple-element.1640, f32[1,256,12,64]{1,0,3,2:T(1,128)S(1)} %copy.376, s32[]{:T(128)S(6)} %sub.537, s32[]{:T(128)} %constant.456.clone.1..sunk.3, s32[]{:T(128)} %constant.456.clone.1..sunk.3, s32[]{:T(128)} %constant.456.clone.1..sunk.3) | dynamic-update-slice | bytes 1572868 | tf_op jit(solution)/shard_map/transpose(jvp())/while/body/jit(dynamic_update_index_in_dim)/dynamic_update_slice | solution.py:112
  477.8 17.9 %dynamic_update_slice.118 = f32[4,256,12,64]{1,0,3,2:T(4,128)} dynamic-update-slice(f32[4,256,12,64]{1,0,3,2:T(4,128)} %get-tuple-element.1640, f32[1,256,12,64]{1,0,3,2:T(1,128)S(1)} %copy.376, s32[]{:T(128)S(6)} %sub.537, s32[]{:T(128)} %constant.456.clone.1..sunk.3, s32[]{:T(128)} %constant.456.clone.1..sunk.3, s32[]{:T(128)} %constant.456.clone.1..sunk.3) | dynamic-update-slice | bytes 1572868 | tf_op jit(solution)/shard_map/transpose(jvp())/while/body/jit(dynamic_update_index_in_dim)/dynamic_update_slice | solution.py:112
  532.6 17.9 %dynamic_update_slice.118 = f32[4,256,12,64]{1,0,3,2:T(4,128)} dynamic-update-slice(f32[4,256,12,64]{1,0,3,2:T(4,128)} %get-tuple-element.1640, f32[1,256,12,64]{1,0,3,2:T(1,128)S(1)} %copy.376, s32[]{:T(128)S(6)} %sub.537, s32[]{:T(128)} %constant.456.clone.1..sunk.3, s32[]{:T(128)} %constant.456.clone.1..sunk.3, s32[]{:T(128)} %constant.456.clone.1..sunk.3) | dynamic-update-slice | bytes 1572868 | tf_op jit(solution)/shard_map/transpose(jvp())/while/body/jit(dynamic_update_index_in_dim)/dynamic_update_slice | solution.py:112
  587.3 17.9 %dynamic_update_slice.118 = f32[4,256,12,64]{1,0,3,2:T(4,128)} dynamic-update-slice(f32[4,256,12,64]{1,0,3,2:T(4,128)} %get-tuple-element.1640, f32[1,256,12,64]{1,0,3,2:T(1,128)S(1)} %copy.376, s32[]{:T(128)S(6)} %sub.537, s32[]{:T(128)} %constant.456.clone.1..sunk.3, s32[]{:T(128)} %constant.456.clone.1..sunk.3, s32[]{:T(128)} %constant.456.clone.1..sunk.3) | dynamic-update-slice | bytes 1572868 | tf_op jit(solution)/shard_map/transpose(jvp())/while/body/jit(dynamic_update_index_in_dim)/dynamic_update_slice | solution.py:112
  651.6 5.3 convolution_convert_fusion.3
  657.0 65.9 %while.71 = (s32[]{:T(128)}, f32[1024,1,64]{0,2,1:T(8,128)S(1)}, f32[1024,1,64]{0,2,1:T(8,128)}, f32[2,512,1,4,64]{1,0,4,3,2:T(2,128)}, s32[2]{0:T(128)S(1)}, /*...) while((s32[]{:T(128)}, f32[1024,1,64]{0,2,1:T(8,128)S(1)}, ...), condition=%wide.region_16.17_spmd.clone, body=%wide.region_14.16_spmd.clone.sunk | while | flops 1377565184 | bytes 122624344 | solution.py:215
  670.9 10.4 %dynamic_update_slice.115 = f32[2,512,1,4,64]{1,0,4,3,2:T(2,128)} dynamic-update-slice(f32[2,512,1,4,64]{1,0,4,3,2:T(2,128)} %get-tuple-element.1692, f32[1,512,1,4,64]{1,0,4,3,2:T(1,128)S(1)} %copy.372, s32[]{:T(128)} %get-tuple-element.1689, s32[]{:T(128)} %constant.456.clone.1..sunk.2, s32[]{:T(128)} %constant.456.clone.1..sunk.2, s32[]{:T(128)} %constant.456.clone.1..sunk.2, ...) | dynamic-update-slice | bytes 1048580 | tf_op jit(solution)/shard_map/while/body/jit(dynamic_update_index_in_dim)/dynamic_update_slice | solution.py:176
  703.7 10.4 %dynamic_update_slice.115 = f32[2,512,1,4,64]{1,0,4,3,2:T(2,128)} dynamic-update-slice(f32[2,512,1,4,64]{1,0,4,3,2:T(2,128)} %get-tuple-element.1692, f32[1,512,1,4,64]{1,0,4,3,2:T(1,128)S(1)} %copy.372, s32[]{:T(128)} %get-tuple-element.1689, s32[]{:T(128)} %constant.456.clone.1..sunk.2, s32[]{:T(128)} %constant.456.clone.1..sunk.2, s32[]{:T(128)} %constant.456.clone.1..sunk.2, ...) | dynamic-update-slice | bytes 1048580 | tf_op jit(solution)/shard_map/while/body/jit(dynamic_update_index_in_dim)/dynamic_update_slice | solution.py:176
  785.1 20.3 %collective-permute-done.27 = bf16[1,8,32,256]{3,2,1,0:T(8,128)(2,1)S(1)} collective-permute-done((bf16[1,8,32,256]{3,2,1,0:T(8,128)(2,1)S(1)}, bf16[1,8,32,256]{3,2,1,0:T(8,128)(2,1)S(1)}, u32[]{:S(2)}, u32[]{:S(2)}) %collective-permute-start.27) | collective-permute-done | bytes 131104 | tf_op jit(solution)/shard_map/ppermute | solution.py:227
  905.2 30.3 %collective-permute-done.12 = f32[8,4,128]{2,0,1:T(8,128)S(1)} collective-permute-done((f32[8,4,128]{2,0,1:T(8,128)S(1)}, f32[8,4,128]{2,0,1:T(8,128)S(1)}, u32[]{:S(2)}, u32[]{:S(2)}) %collective-permute-start.12) | collective-permute-done | bytes 16416 | tf_op jit(solution)/shard_map/ppermute | solution.py:227
  940.1 6.0 collective-permute-done.46
  965.9 10.9 %collective-permute-done.23 = bf16[4,1,64,1536]{3,2,0,1:T(8,128)(2,1)S(1)} collective-permute-done((bf16[4,1,64,1536]{3,2,0,1:T(8,128)(2,1)S(1)}, bf16[4,1,64,1536]{3,2,0,1:T(8,128)(2,1)S(1)}, u32[]{:S(2)}, u32[]{:S(2)}) %collective-permute-start.23) | collective-permute-done | bytes 786464 | tf_op jit(solution)/shard_map/ppermute | solution.py:227
  977.1 10.9 %collective-permute-done.60 = bf16[4,1,64,1024]{3,2,0,1:T(8,128)(2,1)S(1)} collective-permute-done((bf16[4,1,64,1024]{3,2,0,1:T(8,128)(2,1)S(1)}, bf16[4,1,64,1024]{3,2,0,1:T(8,128)(2,1)S(1)}, u32[]{:S(2)}, u32[]{:S(2)}) %collective-permute-start.60) | collective-permute-done | bytes 524320 | tf_op jit(solution)/shard_map/ppermute | solution.py:227
  988.3 10.9 %collective-permute-done.55 = bf16[4,1,64,1024]{3,2,0,1:T(8,128)(2,1)S(1)} collective-permute-done((bf16[4,1,64,1024]{3,2,0,1:T(8,128)(2,1)S(1)}, bf16[4,1,64,1024]{3,2,0,1:T(8,128)(2,1)S(1)}, u32[]{:S(2)}, u32[]{:S(2)}) %collective-permute-start.55) | collective-permute-done | bytes 524320 | tf_op jit(solution)/shard_map/ppermute | solution.py:227
  999.6 9.3 collective-permute-done.50
  1012.7 6.1 collective-permute-done.51
  1019.0 11.1 %collective-permute-done.25 = bf16[1,1,64,1536]{3,2,0,1:T(8,128)(2,1)S(1)} collective-permute-done((bf16[1,1,64,1536]{3,2,0,1:T(8,128)(2,1)S(1)}, bf16[1,1,64,1536]{3,2,0,1:T(8,128)(2,1)S(1)}, u32[]{:S(2)}, u32[]{:S(2)}) %collective-permute-start.25) | collective-permute-done | bytes 196640 | tf_op jit(solution)/shard_map/ppermute | solution.py:227
  (1131 shorter events, 659.5 us)
Async XLA Ops:
  5.4 26.4 %collective-permute-start = (bf16[512,1024]{1,0:T(8,128)(2,1)}, bf16[512,1024]{1,0:T(8,128)(2,1)}, u32[]{:S(2)}, u32[]{:S(2)}) collective-permute-start(bf16[512,1024]{1,0:T(8,128)(2,1)} %fusion.185), channel_id=1, source_target_pairs={{0,16},{16,0},{1,17},{17,1},{2,18},{18,2},{3,19},{19,3},{4,20},{20... | collective-permute-start | bytes 3145736 | tf_op jit(solution)/shard_map/ppermute | solution.py:271
  271.4 23.5 %collective-permute-start.1 = (bf16[512,1024]{1,0:T(8,128)(2,1)}, bf16[512,1024]{1,0:T(8,128)(2,1)}, u32[]{:S(2)}, u32[]{:S(2)}) collective-permute-start(bf16[512,1024]{1,0:T(8,128)(2,1)} %constant_dynamic-slice_fusion.34), channel_id=1, source_target_pairs={{0,16},{16,0},{1,17},{17,1},{2,18},{18,2},{3,19},{19,3},{4,20},{20... | collective-permute-start | bytes 3145736 | tf_op jit(solution)/shard_map/ppermute | solution.py:271
  317.5 563.9 %collective-permute-start.58 = (bf16[16,1,64,1024]{3,2,0,1:T(8,128)(2,1)}, bf16[16,1,64,1024]{3,2,0,1:T(8,128)(2,1)}, u32[]{:S(2)}, u32[]{:S(2)}) collective-permute-start(bf16[16,1,64,1024]{3,2,0,1:T(8,128)(2,1)} %dynamic-slice_bitcast_fusion.7), channel_id=1, source_target_pairs={{0,1},{1,0},{2,3},{3,2},{4,5},{5,4},{6,7},{7,6},{8,9},{9,8},{10,11... | collective-permute-start | bytes 6291464 | tf_op jit(solution)/shard_map/ppermute | solution.py:227
  326.5 24.7 %collective-permute-start.2 = (bf16[512,1024]{1,0:T(8,128)(2,1)S(1)}, bf16[512,1024]{1,0:T(8,128)(2,1)S(1)}, u32[]{:S(2)}, u32[]{:S(2)}) collective-permute-start(bf16[512,1024]{1,0:T(8,128)(2,1)S(1)} %get-tuple-element.1072), channel_id=1, source_target_pairs={{0,16},{16,0},{1,17},{17,1},{2,18},{18,2},{3,19},{19,3},{4,20},{20... | collective-permute-start | bytes 3145736 | tf_op jit(solution)/shard_map/ppermute | solution.py:271
  329.5 563.6 %collective-permute-start.53 = (bf16[16,1,64,1024]{3,2,0,1:T(8,128)(2,1)}, bf16[16,1,64,1024]{3,2,0,1:T(8,128)(2,1)}, u32[]{:S(2)}, u32[]{:S(2)}) collective-permute-start(bf16[16,1,64,1024]{3,2,0,1:T(8,128)(2,1)} %dynamic-slice_bitcast_fusion.8), channel_id=1, source_target_pairs={{0,1},{1,0},{2,3},{3,2},{4,5},{5,4},{6,7},{7,6},{8,9},{9,8},{10,11... | collective-permute-start | bytes 6291464 | tf_op jit(solution)/shard_map/ppermute | solution.py:227
  729.4 130.2 %collective-permute-start.44 = (bf16[8,1,64,768]{3,2,0,1:T(8,128)(2,1)}, bf16[8,1,64,768]{3,2,0,1:T(8,128)(2,1)S(1)}, u32[]{:S(2)}, u32[]{:S(2)}) collective-permute-start(bf16[8,1,64,768]{3,2,0,1:T(8,128)(2,1)} %dynamic-slice_bitcast_fusion.14), channel_id=1, source_target_pairs={{0,1},{1,0},{2,3},{3,2},{4,5},{5,4},{6,7},{7,6},{8,9},{9,8},{10,11... | collective-permute-start | bytes 2359304 | tf_op jit(solution)/shard_map/ppermute | solution.py:227
  730.1 45.8 %collective-permute-start.40 = (bf16[8,1,64,256]{3,2,0,1:T(8,128)(2,1)}, bf16[8,1,64,256]{3,2,0,1:T(8,128)(2,1)}, u32[]{:S(2)}, u32[]{:S(2)}) collective-permute-start(bf16[8,1,64,256]{3,2,0,1:T(8,128)(2,1)} %dynamic-slice_bitcast_fusion.24), channel_id=1, source_target_pairs={{0,1},{1,0},{2,3},{3,2},{4,5},{5,4},{6,7},{7,6},{8,9},{9,8},{10,11... | collective-permute-start | bytes 786440 | tf_op jit(solution)/shard_map/ppermute | solution.py:227
  739.0 6.8 collective-permute-start.36
  746.3 6.4 collective-permute-start.37
  777.5 85.6 %collective-permute-start.3 = (bf16[512,1024]{1,0:T(8,128)(2,1)S(1)}, bf16[512,1024]{1,0:T(8,128)(2,1)S(1)}, u32[]{:S(2)}, u32[]{:S(2)}) collective-permute-start(bf16[512,1024]{1,0:T(8,128)(2,1)S(1)} %constant_dynamic-slice_fusion.33), channel_id=1, source_target_pairs={{0,16},{16,0},{1,17},{17,1},{2,18},{18,2},{3,19},{19,3},{4,20},{20... | collective-permute-start | bytes 3145736 | tf_op jit(solution)/shard_map/ppermute | solution.py:271
  784.4 21.1 %collective-permute-start.27 = (bf16[1,8,32,256]{3,2,1,0:T(8,128)(2,1)S(1)}, bf16[1,8,32,256]{3,2,1,0:T(8,128)(2,1)S(1)}, u32[]{:S(2)}, u32[]{:S(2)}) collective-permute-start(bf16[1,8,32,256]{3,2,1,0:T(8,128)(2,1)S(1)} %dynamic-slice_bitcast_fusion.29), channel_id=1, source_target_pairs={{0,16},{16,0},{1,17},{17,1},{2,18},{18,2},{3,19},{19,3},{4,20},{20... | collective-permute-start | bytes 393224 | tf_op jit(solution)/shard_map/ppermute | solution.py:227
  859.5 41.6 %collective-permute-start.48 = (bf16[16,1,64,1024]{3,2,0,1:T(8,128)(2,1)}, bf16[16,1,64,1024]{3,2,0,1:T(8,128)(2,1)}, u32[]{:S(2)}, u32[]{:S(2)}) collective-permute-start(bf16[16,1,64,1024]{3,2,0,1:T(8,128)(2,1)} %dynamic-slice_bitcast_fusion.9), channel_id=1, source_target_pairs={{0,1},{1,0},{2,3},{3,2},{4,5},{5,4},{6,7},{7,6},{8,9},{9,8},{10,11... | collective-permute-start | bytes 6291464 | tf_op jit(solution)/shard_map/ppermute | solution.py:227
  860.5 93.2 %collective-permute-start.22 = (bf16[8,1,64,1536]{3,2,0,1:T(8,128)(2,1)}, bf16[8,1,64,1536]{3,2,0,1:T(8,128)(2,1)}, u32[]{:S(2)}, u32[]{:S(2)}) collective-permute-start(bf16[8,1,64,1536]{3,2,0,1:T(8,128)(2,1)} %dynamic-slice_bitcast_fusion.10), channel_id=1, source_target_pairs={{0,1},{1,0},{2,3},{3,2},{4,5},{5,4},{6,7},{7,6},{8,9},{9,8},{10,11... | collective-permute-start | bytes 4718600 | tf_op jit(solution)/shard_map/ppermute | solution.py:227
  880.9 58.0 %collective-permute-start.45 = (bf16[4,1,64,768]{3,2,0,1:T(8,128)(2,1)S(1)}, bf16[4,1,64,768]{3,2,0,1:T(8,128)(2,1)S(1)}, u32[]{:S(2)}, u32[]{:S(2)}) collective-permute-start(bf16[4,1,64,768]{3,2,0,1:T(8,128)(2,1)S(1)} %copy-done.92), channel_id=1, source_target_pairs={{0,2},{1,3},{2,0},{3,1},{4,6},{5,7},{6,4},{7,5},{8,10},{9,11},{10,... | collective-permute-start | bytes 1179656 | tf_op jit(solution)/shard_map/ppermute | solution.py:227
  891.6 66.2 %collective-permute-start.59 = (bf16[1,8,64,1024]{3,2,1,0:T(8,128)(2,1)S(1)}, bf16[1,8,64,1024]{3,2,1,0:T(8,128)(2,1)}, u32[]{:S(2)}, u32[]{:S(2)}) collective-permute-start(bf16[1,8,64,1024]{3,2,1,0:T(8,128)(2,1)S(1)} %dynamic-slice_bitcast_fusion.11), channel_id=1, source_target_pairs={{0,16},{16,0},{1,17},{17,1},{2,18},{18,2},{3,19},{19,3},{4,20},{20... | collective-permute-start | bytes 3145736 | tf_op jit(solution)/shard_map/ppermute | solution.py:227
  900.5 59.9 %collective-permute-start.54 = (bf16[1,8,64,1024]{3,2,1,0:T(8,128)(2,1)}, bf16[1,8,64,1024]{3,2,1,0:T(8,128)(2,1)}, u32[]{:S(2)}, u32[]{:S(2)}) collective-permute-start(bf16[1,8,64,1024]{3,2,1,0:T(8,128)(2,1)} %dynamic-slice_bitcast_fusion.12), channel_id=1, source_target_pairs={{0,16},{16,0},{1,17},{17,1},{2,18},{18,2},{3,19},{19,3},{4,20},{20... | collective-permute-start | bytes 3145736 | tf_op jit(solution)/shard_map/ppermute | solution.py:227
  901.1 34.4 %collective-permute-start.12 = (f32[8,4,128]{2,0,1:T(8,128)S(1)}, f32[8,4,128]{2,0,1:T(8,128)S(1)}, u32[]{:S(2)}, u32[]{:S(2)}) collective-permute-start(f32[8,4,128]{2,0,1:T(8,128)S(1)} %bitcast.1090), channel_id=1, source_target_pairs={{0,16},{16,0},{1,17},{17,1},{2,18},{18,2},{3,19},{19,3},{4,20},{20... | collective-permute-start | bytes 49160 | tf_op jit(solution)/shard_map/ppermute | solution.py:227
  936.8 26.9 %collective-permute-start.49 = (bf16[1,8,64,1024]{3,2,1,0:T(8,128)(2,1)}, bf16[1,8,64,1024]{3,2,1,0:T(8,128)(2,1)}, u32[]{:S(2)}, u32[]{:S(2)}) collective-permute-start(bf16[1,8,64,1024]{3,2,1,0:T(8,128)(2,1)} %dynamic-slice_bitcast_fusion.13), channel_id=1, source_target_pairs={{0,16},{16,0},{1,17},{17,1},{2,18},{18,2},{3,19},{19,3},{4,20},{20... | collective-permute-start | bytes 3145736 | tf_op jit(solution)/shard_map/ppermute | solution.py:227
  939.1 7.0 collective-permute-start.46
  946.1 6.9 collective-permute-start.47
  956.2 20.5 %collective-permute-start.23 = (bf16[4,1,64,1536]{3,2,0,1:T(8,128)(2,1)S(1)}, bf16[4,1,64,1536]{3,2,0,1:T(8,128)(2,1)S(1)}, u32[]{:S(2)}, u32[]{:S(2)}) collective-permute-start(bf16[4,1,64,1536]{3,2,0,1:T(8,128)(2,1)S(1)} %dynamic-slice_bitcast_fusion.15), channel_id=1, source_target_pairs={{0,2},{1,3},{2,0},{3,1},{4,6},{5,7},{6,4},{7,5},{8,10},{9,11},{10,... | collective-permute-start | bytes 2359304 | tf_op jit(solution)/shard_map/ppermute | solution.py:227
  959.8 28.2 %collective-permute-start.60 = (bf16[4,1,64,1024]{3,2,0,1:T(8,128)(2,1)S(1)}, bf16[4,1,64,1024]{3,2,0,1:T(8,128)(2,1)S(1)}, u32[]{:S(2)}, u32[]{:S(2)}) collective-permute-start(bf16[4,1,64,1024]{3,2,0,1:T(8,128)(2,1)S(1)} %dynamic-slice_bitcast_fusion.16), channel_id=1, source_target_pairs={{0,2},{1,3},{2,0},{3,1},{4,6},{5,7},{6,4},{7,5},{8,10},{9,11},{10,... | collective-permute-start | bytes 1572872 | tf_op jit(solution)/shard_map/ppermute | solution.py:227
  962.1 37.2 %collective-permute-start.55 = (bf16[4,1,64,1024]{3,2,0,1:T(8,128)(2,1)S(1)}, bf16[4,1,64,1024]{3,2,0,1:T(8,128)(2,1)S(1)}, u32[]{:S(2)}, u32[]{:S(2)}) collective-permute-start(bf16[4,1,64,1024]{3,2,0,1:T(8,128)(2,1)S(1)} %dynamic-slice_bitcast_fusion.17), channel_id=1, source_target_pairs={{0,2},{1,3},{2,0},{3,1},{4,6},{5,7},{6,4},{7,5},{8,10},{9,11},{10,... | collective-permute-start | bytes 1572872 | tf_op jit(solution)/shard_map/ppermute | solution.py:227
  965.3 43.5 %collective-permute-start.50 = (bf16[4,1,64,1024]{3,2,0,1:T(8,128)(2,1)S(1)}, bf16[4,1,64,1024]{3,2,0,1:T(8,128)(2,1)S(1)}, u32[]{:S(2)}, u32[]{:S(2)}) collective-permute-start(bf16[4,1,64,1024]{3,2,0,1:T(8,128)(2,1)S(1)} %dynamic-slice_bitcast_fusion.18), channel_id=1, source_target_pairs={{0,2},{1,3},{2,0},{3,1},{4,6},{5,7},{6,4},{7,5},{8,10},{9,11},{10,... | collective-permute-start | bytes 1572872 | tf_op jit(solution)/shard_map/ppermute | solution.py:227
  977.1 32.1 %collective-permute-start.24 = (bf16[2,1,64,1536]{3,2,0,1:T(8,128)(2,1)S(1)}, bf16[2,1,64,1536]{3,2,0,1:T(8,128)(2,1)S(1)}, u32[]{:S(2)}, u32[]{:S(2)}) collective-permute-start(bf16[2,1,64,1536]{3,2,0,1:T(8,128)(2,1)S(1)} %dynamic-slice_bitcast_fusion.20), channel_id=1, source_target_pairs={{0,4},{1,5},{2,6},{3,7},{4,0},{5,1},{6,2},{7,3},{8,12},{9,13},{10,... | collective-permute-start | bytes 1179656 | tf_op jit(solution)/shard_map/ppermute | solution.py:227
  988.3 21.1 %collective-permute-start.61 = (bf16[2,1,64,1024]{3,2,0,1:T(8,128)(2,1)S(1)}, bf16[2,1,64,1024]{3,2,0,1:T(8,128)(2,1)S(1)}, u32[]{:S(2)}, u32[]{:S(2)}) collective-permute-start(bf16[2,1,64,1024]{3,2,0,1:T(8,128)(2,1)S(1)} %dynamic-slice_bitcast_fusion.21), channel_id=1, source_target_pairs={{0,4},{1,5},{2,6},{3,7},{4,0},{5,1},{6,2},{7,3},{8,12},{9,13},{10,... | collective-permute-start | bytes 786440 | tf_op jit(solution)/shard_map/ppermute | solution.py:227
  999.5 13.0 %collective-permute-start.56 = (bf16[2,1,64,1024]{3,2,0,1:T(8,128)(2,1)S(1)}, bf16[2,1,64,1024]{3,2,0,1:T(8,128)(2,1)S(1)}, u32[]{:S(2)}, u32[]{:S(2)}) collective-permute-start(bf16[2,1,64,1024]{3,2,0,1:T(8,128)(2,1)S(1)} %dynamic-slice_bitcast_fusion.22), channel_id=1, source_target_pairs={{0,4},{1,5},{2,6},{3,7},{4,0},{5,1},{6,2},{7,3},{8,12},{9,13},{10,... | collective-permute-start | bytes 786440 | tf_op jit(solution)/shard_map/ppermute | solution.py:227
  1009.1 9.7 collective-permute-start.51
  1009.3 20.8 %collective-permute-start.25 = (bf16[1,1,64,1536]{3,2,0,1:T(8,128)(2,1)S(1)}, bf16[1,1,64,1536]{3,2,0,1:T(8,128)(2,1)S(1)}, u32[]{:S(2)}, u32[]{:S(2)}) collective-permute-start(bf16[1,1,64,1536]{3,2,0,1:T(8,128)(2,1)S(1)} %constant_dynamic-slice_fusion.19), channel_id=1, source_target_pairs={{0,8},{1,9},{2,10},{3,11},{4,12},{5,13},{6,14},{7,15},{8,0},{9,1},... | collective-permute-start | bytes 589832 | tf_op jit(solution)/shard_map/ppermute | solution.py:227
  1009.5 23.4 %collective-permute-start.62 = (bf16[1,1,64,1024]{3,2,0,1:T(8,128)(2,1)S(1)}, bf16[1,1,64,1024]{3,2,0,1:T(8,128)(2,1)S(1)}, u32[]{:S(2)}, u32[]{:S(2)}) collective-permute-start(bf16[1,1,64,1024]{3,2,0,1:T(8,128)(2,1)S(1)} %constant_dynamic-slice_fusion.3), channel_id=1, source_target_pairs={{0,8},{1,9},{2,10},{3,11},{4,12},{5,13},{6,14},{7,15},{8,0},{9,1},... | collective-permute-start | bytes 393224 | tf_op jit(solution)/shard_map/ppermute | solution.py:227
  1012.6 22.7 %collective-permute-start.57 = (bf16[1,1,64,1024]{3,2,0,1:T(8,128)(2,1)S(1)}, bf16[1,1,64,1024]{3,2,0,1:T(8,128)(2,1)S(1)}, u32[]{:S(2)}, u32[]{:S(2)}) collective-permute-start(bf16[1,1,64,1024]{3,2,0,1:T(8,128)(2,1)S(1)} %constant_dynamic-slice_fusion.4), channel_id=1, source_target_pairs={{0,8},{1,9},{2,10},{3,11},{4,12},{5,13},{6,14},{7,15},{8,0},{9,1},... | collective-permute-start | bytes 393224 | tf_op jit(solution)/shard_map/ppermute | solution.py:227
  1018.9 17.8 %collective-permute-start.52 = (bf16[1,1,64,1024]{3,2,0,1:T(8,128)(2,1)S(1)}, bf16[1,1,64,1024]{3,2,0,1:T(8,128)(2,1)S(1)}, u32[]{:S(2)}, u32[]{:S(2)}) collective-permute-start(bf16[1,1,64,1024]{3,2,0,1:T(8,128)(2,1)S(1)} %constant_dynamic-slice_fusion.5), channel_id=1, source_target_pairs={{0,8},{1,9},{2,10},{3,11},{4,12},{5,13},{6,14},{7,15},{8,0},{9,1},... | collective-permute-start | bytes 393224 | tf_op jit(solution)/shard_map/ppermute | solution.py:227
  (272 other events, 2883.8 us)

commit v2 on v1

v2 whole, which is shorter than its diff:
```python
import functools

import jax
import jax.numpy as jnp
from jax import lax
from jax.experimental import pallas as pl
from jax.experimental.pallas import tpu as pltpu
from jax.sharding import PartitionSpec as P

HD = 64
SH = 24
SP = 64
BLOCK = 256
REACH = 512
EPSILON = 1e-05
ROPE_BASE = 100000000000.0
F32 = jnp.float32
BF16 = jnp.bfloat16
PRECISE = lax.Precision.HIGHEST


def mm(left, right, left_dim, right_dim):
    return lax.dot_general(
        left, right, (((left_dim,), (right_dim,)), ((), ())), preferred_element_type=F32
    )


def mm_exact(left, right):
    return jnp.dot(left, right, preferred_element_type=F32, precision=PRECISE)


def shift_right(prev, cur, amount):
    joined = jnp.concatenate([prev, cur], axis=1)
    return pltpu.roll(joined, amount, 1)[:, prev.shape[1] :]


def shift_left(cur, after, amount):
    joined = jnp.concatenate([cur, after], axis=1)
    total = joined.shape[1]
    return pltpu.roll(joined, total - amount, 1)[:, : cur.shape[1]]


def conv_rows(prev_ref, cur_ref, tap_ref, run_row, is_first):
    cur = cur_ref[...].astype(F32)
    prev = jnp.where(is_first, 0.0, prev_ref[...].astype(F32))
    taps = tap_ref[...]
    result = taps[:, 4:5] + taps[:, 3:4] * cur
    for offset in range(1, 4):
        keep = (run_row >= float(offset)).astype(F32)
        moved = shift_right(prev, cur, offset) * keep
        result = result + taps[:, 3 - offset : 4 - offset] * moved
    return result


def step_rows(step_ref, head_ref):
    raw = step_ref[...] + head_ref[:, 0:1]
    return raw, jax.nn.softplus(raw)


def masks_of(run_col, block):
    rows = lax.broadcasted_iota(jnp.int32, (block, block), 0)
    cols = lax.broadcasted_iota(jnp.int32, (block, block), 1)
    gap = (rows - cols).astype(F32)
    return (gap >= 0.0) & (gap <= run_col)


def upper_ones(block):
    rows = lax.broadcasted_iota(jnp.int32, (block, block), 0)
    cols = lax.broadcasted_iota(jnp.int32, (block, block), 1)
    return (rows <= cols).astype(F32)


def ssd_forward_kernel(
    block, heads, head_dim,
    z_ref, x_ref, xp_ref, b_ref, bp_ref, step_ref, run_ref, runc_ref, tapx_ref, tapb_ref, head_ref, skip_ref,
    gated_ref, entry_ref,
    state, xdt, yrow,
):
    index = pl.program_id(0)
    is_first = index == 0

    @pl.when(is_first)
    def _():
        state[...] = jnp.zeros_like(state)

    run_row = run_ref[0:1, :]
    act = conv_rows(xp_ref, x_ref, tapx_ref, run_row, is_first)
    act = act * jax.nn.sigmoid(act)
    vec = conv_rows(bp_ref, b_ref, tapb_ref, run_row, is_first)
    vec = vec * jax.nn.sigmoid(vec)
    size = vec.shape[0] // 2
    in_low = vec[:size].astype(BF16)
    out_low = vec[size:].astype(BF16)
    raw, step = step_rows(step_ref, head_ref)
    rate = head_ref[:, 1:2]
    cum = mm_exact(step * rate, upper_ones(block))
    cum_col = jnp.transpose(cum)
    place = lax.broadcasted_iota(jnp.int32, (1, block), 1).astype(F32)
    carried = (run_row >= place + 1.0).astype(F32)
    last_run = run_row[:, block - 1 :]
    tail = (float(block - 1) - place <= last_run).astype(F32)
    last = cum[:, block - 1 :]
    entry = jnp.exp(cum) * carried
    to_end = jnp.exp(last - cum) * tail
    keep = jnp.exp(last) * carried[:, block - 1 :]
    allowed = masks_of(runc_ref[:, 0:1], block)
    cross = jnp.where(allowed, mm(out_low, in_low, 0, 0), 0.0)
    old = state[...]
    old_low = old.astype(BF16)
    entry_ref[0] = old_low
    y_off = mm(old_low, out_low, 1, 0)
    for h in range(heads):
        rows = slice(h * head_dim, (h + 1) * head_dim)
        part = act[rows] * step[h : h + 1]
        part_low = part.astype(BF16)
        decay = jnp.exp(jnp.minimum(cum_col[:, h : h + 1] - cum[h : h + 1], 0.0))
        weight = (cross * decay).astype(BF16)
        y_in = mm(part_low, weight, 1, 1)
        yrow[rows] = y_in + y_off[rows] * entry[h : h + 1] + skip_ref[rows, 0:1] * act[rows]
        xdt[rows] = (part * to_end[h : h + 1]).astype(BF16)
        state[rows] = old[rows] * keep[h : h + 1]
    state[...] += mm(xdt[...], in_low, 1, 1)
    gate = z_ref[...].astype(F32)
    gated_ref[...] = (yrow[...] * gate * jax.nn.sigmoid(gate)).astype(gated_ref.dtype)


def ssd_backward_kernel(
    block, heads, head_dim,
    z_ref, x_ref, xp_ref, b_ref, bp_ref, step_ref, run_ref, runc_ref, tapx_ref, tapb_ref, head_ref, skip_ref,
    entry_ref, grad_ref, runn_ref,
    dm_ref, db_ref, dstep_ref, drate_ref, dtapx_ref, dtapb_ref, dskip_ref,
    dstate, nextx, nextb, accx, accb, accs, yrow, dact, xdt, dye, rowterm, colin, colst, direct, ystat,
):
    index = pl.program_id(0)
    count = pl.num_programs(0)
    is_first = index == count - 1

    @pl.when(index == 0)
    def _():
        dstate[...] = jnp.zeros_like(dstate)
        nextx[...] = jnp.zeros_like(nextx)
        nextb[...] = jnp.zeros_like(nextb)
        accx[...] = jnp.zeros_like(accx)
        accb[...] = jnp.zeros_like(accb)
        accs[...] = jnp.zeros_like(accs)
        rowterm[...] = jnp.zeros_like(rowterm)
        colin[...] = jnp.zeros_like(colin)
        colst[...] = jnp.zeros_like(colst)
        direct[...] = jnp.zeros_like(direct)
        ystat[...] = jnp.zeros_like(ystat)

    run_row = run_ref[0:1, :]
    convx = conv_rows(xp_ref, x_ref, tapx_ref, run_row, is_first)
    sigx = jax.nn.sigmoid(convx)
    act = convx * sigx
    convb = conv_rows(bp_ref, b_ref, tapb_ref, run_row, is_first)
    sigb = jax.nn.sigmoid(convb)
    vec = convb * sigb
    size = vec.shape[0] // 2
    in_low = vec[:size].astype(BF16)
    out_low = vec[size:].astype(BF16)
    raw, step = step_rows(step_ref, head_ref)
    rate = head_ref[:, 1:2]
    upper = upper_ones(block)
    cum = mm_exact(step * rate, upper)
    cum_col = jnp.transpose(cum)
    place = lax.broadcasted_iota(jnp.int32, (1, block), 1).astype(F32)
    carried = (run_row >= place + 1.0).astype(F32)
    last_run = run_row[:, block - 1 :]
    tail = (float(block - 1) - place <= last_run).astype(F32)
    last = cum[:, block - 1 :]
    entry = jnp.exp(cum) * carried
    to_end = jnp.exp(last - cum) * tail
    keep = jnp.exp(last) * carried[:, block - 1 :]
    allowed = masks_of(runc_ref[:, 0:1], block)
    cross = jnp.where(allowed, mm(out_low, in_low, 0, 0), 0.0)
    old_low = entry_ref[0]
    old = old_low.astype(F32)
    dnew = dstate[...]
    dnew_low = dnew.astype(BF16)
    y_off = mm(old_low, out_low, 1, 0)
    u_off = mm(dnew_low, in_low, 1, 0)
    gate = z_ref[...].astype(F32)
    sig = jax.nn.sigmoid(gate)
    upstream = grad_ref[...].astype(F32)
    dy = upstream * gate * sig
    dcross = jnp.zeros((block, block), F32)
    for h in range(heads):
        rows = slice(h * head_dim, (h + 1) * head_dim)
        one = slice(h, h + 1)
        xh = act[rows]
        part = xh * step[one]
        part_low = part.astype(BF16)
        dyh = dy[rows]
        dy_low = dyh.astype(BF16)
        decay = jnp.exp(jnp.minimum(cum_col[:, one] - cum[one], 0.0))
        weight = (cross * decay).astype(BF16)
        y_in = mm(part_low, weight, 1, 1)
        y_scan = y_in + y_off[rows] * entry[one]
        u_in = mm(dy_low, weight, 1, 0)
        u_st = u_off[rows] * to_end[one]
        dcross = dcross + mm(dy_low, part_low, 0, 0) * decay
        part_f = part_low.astype(F32)
        u_all = u_in + u_st
        rowterm[one] = jnp.sum(dy_low.astype(F32) * y_scan, axis=0, keepdims=True)
        colin[one] = jnp.sum(part_f * u_in, axis=0, keepdims=True)
        colst[one] = jnp.sum(part_f * u_st, axis=0, keepdims=True)
        direct[one] = jnp.sum(xh * u_all, axis=0, keepdims=True)
        skip = skip_ref[rows, 0:1]
        yrow[rows] = y_scan + skip * xh
        dact[rows] = step[one] * u_all + skip * dyh
        xdt[rows] = (part * to_end[one]).astype(BF16)
        dye[rows] = (dyh * entry[one]).astype(BF16)
        kept = jnp.sum(dnew[rows] * old[rows] * keep[one], axis=0, keepdims=True)
        ystat[one] = kept
        dstate[rows] = dnew[rows] * keep[one]
    dcross_low = jnp.where(allowed, dcross, 0.0).astype(BF16)
    dout = mm(in_low, dcross_low, 1, 1) + mm(old_low, dye[...], 0, 0)
    din = mm(out_low, dcross_low, 1, 0) + mm(dnew_low, xdt[...], 0, 0)
    dstate[...] += mm(dye[...], out_low, 1, 1)
    inner = upstream.shape[0]
    dm_ref[:inner] = (upstream * yrow[...] * sig * (1.0 + gate * (1.0 - sig))).astype(dm_ref.dtype)
    prod = dy * act
    accs[...] += sum(prod[:, c : c + 128] for c in range(0, block, 128))
    lower = jnp.transpose(upper)
    kept_total = jnp.sum(ystat[...], axis=1, keepdims=True)
    dlog = (
        mm_exact(rowterm[...] - colin[...], lower)
        + mm_exact(colst[...], upper)
        - colst[...]
        + kept_total
    )
    dstep = direct[...] + rate * dlog
    dstep_ref[...] = dstep * jax.nn.sigmoid(raw)
    drate_ref[...] = dlog * step

    def conv_back(dvals, conv, sigm, prev_ref, cur_ref, tap_ref, after, acc, out_ref):
        dconv = dvals * sigm * (1.0 + conv * (1.0 - sigm))
        taps = tap_ref[...]
        cur = cur_ref[...].astype(F32)
        prev = jnp.where(is_first, 0.0, prev_ref[...].astype(F32))
        result = taps[:, 3:4] * dconv
        acc[4] += sum(dconv[:, c : c + 128] for c in range(0, block, 128))
        prod = dconv * cur
        acc[3] += sum(prod[:, c : c + 128] for c in range(0, block, 128))
        following = after[...]
        for offset in range(1, 4):
            keep_cur = (run_row >= float(offset)).astype(F32)
            keep_next = (runn_ref[0:1, :] >= float(offset)).astype(F32)
            masked = dconv * keep_cur
            result = result + taps[:, 3 - offset : 4 - offset] * shift_left(
                masked, following * keep_next, offset
            )
            prod = masked * shift_right(prev, cur, offset)
            acc[3 - offset] += sum(prod[:, c : c + 128] for c in range(0, block, 128))
        after[...] = dconv[:, :128]
        out_ref[...] = result.astype(out_ref.dtype)

    conv_back(dact[...], convx, sigx, xp_ref, x_ref, tapx_ref, nextx, accx, dm_ref.at[inner:])
    conv_back(
        jnp.concatenate([din, dout], axis=0), convb, sigb, bp_ref, b_ref, tapb_ref, nextb, accb, db_ref
    )

    @pl.when(is_first)
    def _():
        def spread(acc, out_ref):
            lanes = lax.broadcasted_iota(jnp.int32, out_ref.shape, 1)
            result = jnp.zeros(out_ref.shape, F32)
            for item in range(5):
                total = jnp.sum(acc[item], axis=1, keepdims=True)
                result = jnp.where(lanes == item, total, result)
            out_ref[...] = result

        spread(accx, dtapx_ref)
        spread(accb, dtapb_ref)
        dskip_ref[...] = jnp.broadcast_to(
            jnp.sum(accs[...], axis=1, keepdims=True), dskip_ref.shape
        )


def ssd_specs(block, inner, vec, rows16, chunk_of):
    wide = lambda i: (0, chunk_of(i))
    per = block // 128
    before = lambda i: (0, jnp.maximum(chunk_of(i) * per - 1, 0))
    whole = lambda i: (0, 0)
    return [
        pl.BlockSpec((inner, block), wide),
        pl.BlockSpec((inner, block), lambda i: (1, chunk_of(i))),
        pl.BlockSpec((inner, 128), lambda i: (1, before(i)[1])),
        pl.BlockSpec((vec, block), wide),
        pl.BlockSpec((vec, 128), before),
        pl.BlockSpec((rows16, block), wide),
        pl.BlockSpec((8, block), wide),
        pl.BlockSpec((block, 128), lambda i: (chunk_of(i), 0)),
        pl.BlockSpec((inner, 128), whole),
        pl.BlockSpec((vec, 128), whole),
        pl.BlockSpec((rows16, 128), whole),
        pl.BlockSpec((inner, 128), whole),
    ]


def ssd_forward(mixer_t, vec_t, step_t, run8, run_col, tap_x, tap_b, head_cols, skip_col, heads, head_dim, block):
    inner = mixer_t.shape[0] // 2
    seq = mixer_t.shape[1]
    vec = vec_t.shape[0]
    rows16 = step_t.shape[0]
    chunks = seq // block
    state_dim = vec // 2
    return pl.pallas_call(
        functools.partial(ssd_forward_kernel, block, heads, head_dim),
        grid=(chunks,),
        in_specs=ssd_specs(block, inner, vec, rows16, lambda i: i),
        out_specs=[
            pl.BlockSpec((inner, block), lambda i: (0, i)),
            pl.BlockSpec((1, inner, state_dim), lambda i: (i, 0, 0)),
        ],
        out_shape=[
            jax.ShapeDtypeStruct((inner, seq), BF16),
            jax.ShapeDtypeStruct((chunks, inner, state_dim), BF16),
        ],
        scratch_shapes=[
            pltpu.VMEM((inner, state_dim), F32),
            pltpu.VMEM((inner, block), BF16),
            pltpu.VMEM((inner, block), F32),
        ],
        compiler_params=pltpu.CompilerParams(vmem_limit_bytes=48 << 20),
        cost_estimate=pl.CostEstimate(flops=10**9, bytes_accessed=10**7, transcendentals=10**7),
        name="ssd_forward",
    )(mixer_t, mixer_t, mixer_t, vec_t, vec_t, step_t, run8, run_col, tap_x, tap_b, head_cols, skip_col)


def ssd_backward(mixer_t, vec_t, step_t, run8, run_col, tap_x, tap_b, head_cols, skip_col, entry, grad_t, heads, head_dim, block):
    inner = mixer_t.shape[0] // 2
    seq = mixer_t.shape[1]
    vec = vec_t.shape[0]
    rows16 = step_t.shape[0]
    chunks = seq // block
    state_dim = vec // 2
    per = block // 128
    chunk_of = lambda i: chunks - 1 - i
    wide = lambda i: (0, chunk_of(i))
    whole = lambda i: (0, 0)
    return pl.pallas_call(
        functools.partial(ssd_backward_kernel, block, heads, head_dim),
        grid=(chunks,),
        in_specs=ssd_specs(block, inner, vec, rows16, chunk_of)
        + [
            pl.BlockSpec((1, inner, state_dim), lambda i: (chunk_of(i), 0, 0)),
            pl.BlockSpec((inner, block), wide),
            pl.BlockSpec((8, 128), lambda i: (0, jnp.minimum(chunk_of(i) * per + per, chunks * per - 1))),
        ],
        out_specs=[
            pl.BlockSpec((2 * inner, block), wide),
            pl.BlockSpec((vec, block), wide),
            pl.BlockSpec((rows16, block), wide),
            pl.BlockSpec((rows16, block), wide),
            pl.BlockSpec((inner, 128), whole),
            pl.BlockSpec((vec, 128), whole),
            pl.BlockSpec((inner, 128), whole),
        ],
        out_shape=[
            jax.ShapeDtypeStruct((2 * inner, seq), BF16),
            jax.ShapeDtypeStruct((vec, seq), BF16),
            jax.ShapeDtypeStruct((rows16, seq), F32),
            jax.ShapeDtypeStruct((rows16, seq), F32),
            jax.ShapeDtypeStruct((inner, 128), F32),
            jax.ShapeDtypeStruct((vec, 128), F32),
            jax.ShapeDtypeStruct((inner, 128), F32),
        ],
        scratch_shapes=[
            pltpu.VMEM((inner, state_dim), F32),
            pltpu.VMEM((inner, 128), F32),
            pltpu.VMEM((vec, 128), F32),
            pltpu.VMEM((5, inner, 128), F32),
            pltpu.VMEM((5, vec, 128), F32),
            pltpu.VMEM((inner, 128), F32),
            pltpu.VMEM((inner, block), F32),
            pltpu.VMEM((inner, block), F32),
            pltpu.VMEM((inner, block), BF16),
            pltpu.VMEM((inner, block), BF16),
            pltpu.VMEM((rows16, block), F32),
            pltpu.VMEM((rows16, block), F32),
            pltpu.VMEM((rows16, block), F32),
            pltpu.VMEM((rows16, block), F32),
            pltpu.VMEM((rows16, state_dim), F32),
        ],
        compiler_params=pltpu.CompilerParams(vmem_limit_bytes=48 << 20),
        cost_estimate=pl.CostEstimate(flops=3 * 10**9, bytes_accessed=2 * 10**7, transcendentals=3 * 10**7),
        name="ssd_backward",
    )(
        mixer_t, mixer_t, mixer_t, vec_t, vec_t, step_t, run8, run_col, tap_x, tap_b, head_cols, skip_col,
        entry, grad_t, run8,
    )


def rotate_rows(values, cosine, sine):
    half = values.shape[0] // 2
    first, second = values[:half], values[half:]
    return jnp.concatenate(
        [first * cosine - second * sine, second * cosine + first * sine], axis=0
    )


def window_of(block_index, block, reach):
    low = max(0, (block_index * block - (reach - 1)) // block)
    return low * block, (block_index + 1) * block


def allowed_of(run_ref, begin, stop, block):
    start, end = stop
    keys = lax.broadcasted_iota(jnp.int32, (end - start, block), 0) + start
    queries = lax.broadcasted_iota(jnp.int32, (end - start, block), 1) + begin
    gap = (queries - keys).astype(F32)
    return (gap >= 0.0) & (gap <= run_ref[0:1, begin : begin + block])


def attention_forward_kernel(
    heads, groups, head_dim, block, reach, scale,
    proj_ref, cos_ref, sin_ref, run_ref, out_ref, rot_ref, lse_ref,
):
    seq = proj_ref.shape[1]
    cosine, sine = cos_ref[...], sin_ref[...]
    total = heads + groups
    for item in range(total):
        rows = slice(item * head_dim, (item + 1) * head_dim)
        rot_ref[rows] = rotate_rows(proj_ref[rows].astype(F32), cosine, sine).astype(BF16)
    for index in range(seq // block):
        begin = index * block
        span = window_of(index, block, reach)
        allowed = allowed_of(run_ref, begin, span, block)
        for h in range(heads):
            group = h * groups // heads
            rows = slice(h * head_dim, (h + 1) * head_dim)
            krows = slice((heads + group) * head_dim, (heads + group + 1) * head_dim)
            vrows = slice((heads + groups + group) * head_dim, (heads + groups + group + 1) * head_dim)
            query = rot_ref[rows, begin : begin + block]
            key = rot_ref[krows, span[0] : span[1]]
            value = proj_ref[vrows, span[0] : span[1]].astype(BF16)
            logits = jnp.where(allowed, mm(key, query, 0, 0) * scale, -1e30)
            peak = jnp.max(logits, axis=0, keepdims=True)
            powered = jnp.exp(logits - peak)
            mass = jnp.sum(powered, axis=0, keepdims=True)
            probs = (powered * (1.0 / mass)).astype(BF16)
            out_ref[rows, begin : begin + block] = mm(value, probs, 1, 0).astype(out_ref.dtype)
            lse_ref[h : h + 1, begin : begin + block] = peak + jnp.log(mass)


def attention_backward_kernel(
    heads, groups, head_dim, block, reach, scale,
    proj_ref, rot_ref, cos_ref, sin_ref, run_ref, lse_ref, out_in_ref, grad_ref, back_ref,
    acc_key, acc_value,
):
    seq = proj_ref.shape[1]
    acc_key[...] = jnp.zeros_like(acc_key)
    acc_value[...] = jnp.zeros_like(acc_value)
    for index in range(seq // block):
        begin = index * block
        span = window_of(index, block, reach)
        allowed = allowed_of(run_ref, begin, span, block)
        cosine, sine = cos_ref[:, begin : begin + block], sin_ref[:, begin : begin + block]
        for h in range(heads):
            group = h * groups // heads
            rows = slice(h * head_dim, (h + 1) * head_dim)
            krows = slice((heads + group) * head_dim, (heads + group + 1) * head_dim)
            vrows = slice((heads + groups + group) * head_dim, (heads + groups + group + 1) * head_dim)
            grows = slice(group * head_dim, (group + 1) * head_dim)
            query = rot_ref[rows, begin : begin + block]
            key = rot_ref[krows, span[0] : span[1]]
            value = proj_ref[vrows, span[0] : span[1]].astype(BF16)
            grad = grad_ref[rows, begin : begin + block]
            logits = jnp.where(allowed, mm(key, query, 0, 0) * scale, -1e30)
            probs = jnp.exp(logits - lse_ref[h : h + 1, begin : begin + block])
            dprobs = mm(value, grad, 0, 0)
            centre = jnp.sum(probs * dprobs, axis=0, keepdims=True)
            dscore = (probs * (dprobs - centre) * scale).astype(BF16)
            dquery = mm(key, dscore, 1, 0)
            back_ref[rows, begin : begin + block] = rotate_rows(dquery, cosine, -sine).astype(BF16)
            acc_key[grows, span[0] : span[1]] += mm(query, dscore, 1, 1)
            acc_value[grows, span[0] : span[1]] += mm(grad, probs.astype(BF16), 1, 1)
    for group in range(groups):
        grows = slice(group * head_dim, (group + 1) * head_dim)
        krows = slice((heads + group) * head_dim, (heads + group + 1) * head_dim)
        vrows = slice((heads + groups + group) * head_dim, (heads + groups + group + 1) * head_dim)
        back_ref[krows] = rotate_rows(acc_key[grows], cos_ref[...], -sin_ref[...]).astype(BF16)
        back_ref[vrows] = acc_value[grows].astype(BF16)


def attention_forward(proj_t, cosine, sine, run8, heads, groups, head_dim, block, reach):
    seq = proj_t.shape[1]
    return pl.pallas_call(
        functools.partial(attention_forward_kernel, heads, groups, head_dim, block, reach, head_dim**-0.5),
        out_shape=[
            jax.ShapeDtypeStruct((heads * head_dim, seq), BF16),
            jax.ShapeDtypeStruct(((heads + groups) * head_dim, seq), BF16),
            jax.ShapeDtypeStruct((max(heads, 8), seq), F32),
        ],
        compiler_params=pltpu.CompilerParams(vmem_limit_bytes=48 << 20),
        cost_estimate=pl.CostEstimate(flops=2 * 10**9, bytes_accessed=10**7, transcendentals=4 * 10**6),
        name="attention_forward",
    )(proj_t, cosine, sine, run8)


def attention_backward(proj_t, rot_t, cosine, sine, run8, lse, out_t, grad_t, heads, groups, head_dim, block, reach):
    seq = proj_t.shape[1]
    return pl.pallas_call(
        functools.partial(attention_backward_kernel, heads, groups, head_dim, block, reach, head_dim**-0.5),
        out_shape=jax.ShapeDtypeStruct(proj_t.shape, BF16),
        scratch_shapes=[
            pltpu.VMEM((groups * head_dim, seq), F32),
            pltpu.VMEM((groups * head_dim, seq), F32),
        ],
        compiler_params=pltpu.CompilerParams(vmem_limit_bytes=48 << 20),
        cost_estimate=pl.CostEstimate(flops=5 * 10**9, bytes_accessed=10**7, transcendentals=4 * 10**6),
        name="attention_backward",
    )(proj_t, rot_t, cosine, sine, run8, lse, out_t, grad_t)


def ffn_kernel(norm_ref, cot_ref, gate_ref, up_ref, down_ref, out_ref, back_ref, act_ref, dgate_ref, dup_ref):
    @pl.when(pl.program_id(0) == 0)
    def _():
        out_ref[...] = jnp.zeros_like(out_ref)
        back_ref[...] = jnp.zeros_like(back_ref)

    normed, cot = norm_ref[...], cot_ref[...]
    gate_w, up_w, down_w = gate_ref[...], up_ref[...], down_ref[...]
    gate = mm(normed, gate_w, 1, 0)
    up = mm(normed, up_w, 1, 0)
    grad_act = mm(cot, down_w, 1, 1)
    sig = jax.nn.sigmoid(gate)
    silu = gate * sig
    act = (silu * up).astype(BF16)
    dgate = (grad_act * up * sig * (1.0 + gate * (1.0 - sig))).astype(BF16)
    dup = (grad_act * silu).astype(BF16)
    act_ref[...] = act
    dgate_ref[...] = dgate
    dup_ref[...] = dup
    out_ref[...] += mm(act, down_w, 1, 0)
    back_ref[...] += mm(dgate, gate_w, 1, 1) + mm(dup, up_w, 1, 1)


def feed_forward(normed, cot, gate_w, up_w, down_w, tile):
    rows, width = normed.shape
    hidden = gate_w.shape[1]
    whole = lambda i: (0, 0)
    return pl.pallas_call(
        ffn_kernel,
        grid=(hidden // tile,),
        in_specs=[
            pl.BlockSpec((rows, width), whole),
            pl.BlockSpec((rows, width), whole),
            pl.BlockSpec((width, tile), lambda i: (0, i)),
            pl.BlockSpec((width, tile), lambda i: (0, i)),
            pl.BlockSpec((tile, width), lambda i: (i, 0)),
        ],
        out_specs=[
            pl.BlockSpec((rows, width), whole),
            pl.BlockSpec((rows, width), whole),
            pl.BlockSpec((rows, tile), lambda i: (0, i)),
            pl.BlockSpec((rows, tile), lambda i: (0, i)),
            pl.BlockSpec((rows, tile), lambda i: (0, i)),
        ],
        out_shape=[
            jax.ShapeDtypeStruct((rows, width), F32),
            jax.ShapeDtypeStruct((rows, width), F32),
            jax.ShapeDtypeStruct((rows, hidden), BF16),
            jax.ShapeDtypeStruct((rows, hidden), BF16),
            jax.ShapeDtypeStruct((rows, hidden), BF16),
        ],
        compiler_params=pltpu.CompilerParams(vmem_limit_bytes=48 << 20),
        cost_estimate=pl.CostEstimate(flops=6 * 2 * rows * width * hidden, bytes_accessed=3 * 10**7, transcendentals=rows * hidden),
        name="feed_forward",
    )(normed, cot, gate_w, up_w, down_w)


def ffn_wgrad_kernel(norm_ref, cot_ref, act_ref, dgate_ref, dup_ref, gate_ref, up_ref, down_ref):
    normed, cot = norm_ref[...], cot_ref[...]
    gate_ref[...] = mm(dgate_ref[...], normed, 0, 0).astype(BF16)
    up_ref[...] = mm(dup_ref[...], normed, 0, 0).astype(BF16)
    down_ref[...] = mm(act_ref[...], cot, 0, 0).astype(BF16)


def ffn_wgrads(normed, cot, act, dgate, dup, tile):
    rows, width = normed.shape
    hidden = act.shape[1]
    whole = lambda i: (0, 0)
    return pl.pallas_call(
        ffn_wgrad_kernel,
        grid=(hidden // tile,),
        in_specs=[pl.BlockSpec((rows, width), whole)] * 2
        + [pl.BlockSpec((rows, tile), lambda i: (0, i))] * 3,
        out_specs=[pl.BlockSpec((tile, width), lambda i: (i, 0))] * 3,
        out_shape=[jax.ShapeDtypeStruct((hidden, width), BF16)] * 3,
        compiler_params=pltpu.CompilerParams(vmem_limit_bytes=48 << 20),
        cost_estimate=pl.CostEstimate(flops=3 * 2 * rows * width * hidden, bytes_accessed=2 * 10**7, transcendentals=0),
        name="ffn_wgrads",
    )(normed, cot, act, dgate, dup)


def bits_of(count):
    return count.bit_length() - 1


def swap_halves(values, axis_name, bit, size):
    pairs = [(item, item ^ (1 << bit)) for item in range(size)]
    return lax.ppermute(values, axis_name, pairs)


def halve(values, place, my_bit, axis_name, bit, size):
    owners = values.shape[0]
    high = 1 << place
    parts = values.reshape((high, 2, owners // (2 * high)) + values.shape[1:])
    sent = lax.dynamic_index_in_dim(parts, 1 - my_bit, 1, keepdims=False)
    kept = lax.dynamic_index_in_dim(parts, my_bit, 1, keepdims=False)
    got = swap_halves(sent, axis_name, bit, size)
    total = (kept.astype(jnp.float32) + got.astype(jnp.float32)).astype(values.dtype)
    return total.reshape((owners // 2,) + values.shape[1:])


def scatter_sum(values, digits, order):
    left = list(digits)
    for digit in order:
        axis_name, bit, size = digit
        my_bit = (lax.axis_index(axis_name) >> bit) & 1
        values = halve(values, left.index(digit), my_bit, axis_name, bit, size)
        left.remove(digit)
    return values[0]


def gather_all(values, digits, order):
    values = values[None]
    left = []
    for digit in order:
        axis_name, bit, size = digit
        my_bit = (lax.axis_index(axis_name) >> bit) & 1
        got = swap_halves(values, axis_name, bit, size)
        place = sum(1 for item in left if digits.index(item) < digits.index(digit))
        high = 1 << place
        owners = values.shape[0]
        mine = values.reshape((high, 1, owners // high) + values.shape[1:])
        other = got.reshape(mine.shape)
        first = jnp.where(my_bit == 0, mine, other)
        second = jnp.where(my_bit == 0, other, mine)
        values = jnp.concatenate([first, second], axis=1).reshape((owners * 2,) + values.shape[1:])
        left.append(digit)
    return values


def other_branch(values):
    return lax.ppermute(values, "branch", [(0, 1), (1, 0)])


def rms_scale(values):
    return lax.rsqrt(jnp.mean(values * values, axis=-1, keepdims=True) + EPSILON)


def rms_back(upstream, values, scales, gain):
    weighted = upstream * gain
    return scales * weighted - values * scales**3 * jnp.mean(
        weighted * values, axis=-1, keepdims=True
    )


def token_runs(length_row, seq_len, doc_count):
    order = jnp.arange(doc_count, dtype=jnp.int32)
    ends = jnp.sum(jnp.where(order[:, None] >= order[None, :], length_row[None, :], 0), axis=1)
    places = jnp.arange(seq_len, dtype=jnp.int32)
    passed = places[:, None] >= ends[None, :]
    starts = jnp.sum(jnp.where(passed, length_row[None, :], 0), axis=1)
    return (places - starts).astype(F32), jnp.sum(length_row)


def join(mine, other, branch_pos, axis):
    return jnp.concatenate(
        [jnp.where(branch_pos == 0, mine, other), jnp.where(branch_pos == 0, other, mine)], axis=axis
    )


def columns_of(items, rows):
    stacked = jnp.stack(items, axis=1)
    return jnp.pad(stacked, ((0, rows - stacked.shape[0]), (0, 128 - stacked.shape[1])))


def per_device(
    inputs,
    lengths,
    norm_gain,
    query_weight,
    keyval_weight,
    mixer_weight,
    state_weight,
    step_weight,
    conv_mixer,
    conv_state,
    bias_mixer,
    bias_state,
    step_bias,
    decay_log,
    skip_gain,
    ssd_gain,
    attn_output,
    ssd_output,
    ffn_gain,
    gate_weight,
    up_weight,
    down_weight,
    cotangent,
):
    branch_pos = lax.axis_index("branch")
    row_pos = lax.axis_index("rows")
    row_count = lax.axis_size("rows")
    row_bits = bits_of(row_count)
    row_digits = [("rows", bit, row_count) for bit in range(row_bits - 1, -1, -1)]
    branch_digit = ("branch", 0, 2)
    all_digits = [branch_digit] + row_digits
    upward = row_digits[::-1]
    turned = upward[:1] + upward[2:] + upward[1:2]
    order_a = upward + [branch_digit]
    order_b = turned + [branch_digit]
    order_c = upward[:1] + [branch_digit] + upward[1:]

    own_rows = inputs[0].astype(F32)
    upstream = cotangent[0]
    half_len, model_dim = own_rows.shape
    seq_len = 2 * half_len
    local_query = query_weight.shape[1] // HD
    local_keyval = keyval_weight.shape[2] // HD
    local_heads = step_bias.shape[0]
    local_inner = bias_mixer.shape[0]
    inner_dim = 2 * local_inner
    head_rows = -(-local_heads // 8) * 8
    own_begin = branch_pos * half_len

    run, used = token_runs(lengths[0], seq_len, lengths.shape[1])
    run8 = jnp.broadcast_to(run[None, :], (8, seq_len))
    run_col = jnp.broadcast_to(run[:, None], (seq_len, 128))
    frequency = ROPE_BASE ** (-(jnp.arange(HD // 2, dtype=F32) * 2.0) / HD)
    angles = frequency[:, None] * run[None, :]
    cosine, sine = jnp.cos(angles), jnp.sin(angles)
    own_valid = (own_begin + jnp.arange(half_len, dtype=jnp.int32) < used).astype(F32)[:, None]

    own_scale = rms_scale(own_rows)
    own_hat = own_rows * own_scale
    normed = (own_hat * norm_gain).astype(BF16)
    full_normed = join(normed, other_branch(normed), branch_pos, 0)

    qkv_flat = jnp.concatenate([query_weight, keyval_weight.reshape(model_dim, -1)], axis=1)
    mixer_flat = mixer_weight.reshape(model_dim, -1)
    state_flat = state_weight.reshape(model_dim, -1)
    step_flat = jnp.pad(step_weight, ((0, 0), (0, head_rows - local_heads)))

    mixer_t = mm(mixer_flat, full_normed, 0, 1).astype(BF16)
    vec_t = mm(state_flat, full_normed, 0, 1).astype(BF16)
    qkv_t = mm(qkv_flat, full_normed, 0, 1).astype(BF16)
    step_t = mm(step_flat, full_normed, 0, 1)

    taps = [conv_mixer[item] for item in range(4)] + [bias_mixer]
    tap_x = columns_of(taps, local_inner)
    state_taps = [conv_state[item].reshape(-1) for item in range(4)] + [bias_state.reshape(-1)]
    tap_b = columns_of(state_taps, state_flat.shape[1])
    rates = -jnp.exp(decay_log)
    head_cols = columns_of([step_bias, rates], head_rows)
    skip_col = jnp.broadcast_to(jnp.repeat(skip_gain, SP)[:, None], (local_inner, 128))
    ssd_args = (mixer_t, vec_t, step_t, run8, run_col, tap_x, tap_b, head_cols, skip_col)

    gated_t, entry = ssd_forward(*ssd_args, local_heads, SP, BLOCK)
    attn_t, rot_t, log_sums = attention_forward(
        qkv_t, cosine, sine, run8, local_query, local_keyval, HD, BLOCK, REACH
    )

    def own_tokens(values, pos):
        return lax.dynamic_slice_in_dim(values, pos * half_len, half_len, 1)

    def to_owner(values):
        got = other_branch(own_tokens(values, 1 - branch_pos))
        return join(own_tokens(values, branch_pos), got, branch_pos, 0)

    def own_channels(values, pos):
        size = values.shape[0] // 2
        return lax.dynamic_slice_in_dim(values, pos * size, size, 0)

    def to_heads(values):
        got = other_branch(own_channels(values, 1 - branch_pos))
        return join(own_channels(values, branch_pos), got, branch_pos, 1)

    all_gated = to_owner(gated_t)
    all_attn = to_owner(attn_t)
    attn_full = join(attn_output, other_branch(attn_output), branch_pos, 0)
    ssd_full = join(ssd_output, other_branch(ssd_output), branch_pos, 0)
    gain_full = join(ssd_gain, other_branch(ssd_gain), branch_pos, 0)[:, None]

    gated = all_gated.astype(F32)
    gated_scale = lax.rsqrt(jnp.mean(gated * gated, axis=0, keepdims=True) + EPSILON)
    ssd_low = (gated * gated_scale * gain_full).astype(BF16)
    mixer_sum = mm(all_attn, attn_full, 0, 0) + mm(ssd_low, ssd_full, 0, 0)
    hidden = own_rows + own_valid * mixer_sum
    hidden_scale = rms_scale(hidden)
    hidden_hat = hidden * hidden_scale
    normed_ffn = (hidden_hat * ffn_gain).astype(BF16)

    ffn_out, grad_normed_ffn, act_low, grad_gate, grad_up = feed_forward(
        normed_ffn, upstream, gate_weight, up_weight, down_weight, 256
    )
    block_out = (hidden + ffn_out).astype(BF16)[None]
    grad_hidden = upstream.astype(F32) + rms_back(grad_normed_ffn, hidden, hidden_scale, ffn_gain)
    ffn_gain_grad = jnp.sum(grad_normed_ffn * hidden_hat, axis=0)
    grad_mixer = (own_valid * grad_hidden).astype(BF16)

    grad_attn = mm(attn_full, grad_mixer, 1, 1).astype(BF16)
    grad_ssd = mm(ssd_full, grad_mixer, 1, 1)
    ssd_gain_wgrad = jnp.sum(grad_ssd * gated * gated_scale, axis=1)
    weighted = grad_ssd * gain_full
    row_inner = jnp.mean(weighted * gated, axis=0, keepdims=True)
    grad_gated = (gated_scale * weighted - gated * gated_scale**3 * row_inner).astype(BF16)
    head_gated = to_heads(grad_gated)
    head_attn = to_heads(grad_attn)

    gate_wgrad, up_wgrad, down_wgrad = ffn_wgrads(
        normed_ffn, upstream, act_low, grad_gate, grad_up, 512
    )

    def owner_rows(partial):
        return partial.reshape((2 * row_count, -1) + partial.shape[1:])

    ffn_sums = [
        scatter_sum(owner_rows(item), all_digits, order)
        for item, order in ((gate_wgrad, order_a), (up_wgrad, order_b), (down_wgrad, order_c))
    ]
    ffn_grads = (
        ffn_sums[0].astype(F32).T,
        ffn_sums[1].astype(F32).T,
        ffn_sums[2].astype(F32),
    )

    def out_wgrad(channels, order):
        parts = [
            mm(grad_mixer, own_channels(channels, pos), 0, 1).astype(BF16) for pos in (0, 1)
        ]
        stacked = jnp.stack(parts)
        return scatter_sum(owner_rows(stacked.reshape((-1,) + stacked.shape[2:])), all_digits, order)

    attn_out_sum = out_wgrad(all_attn, order_a).astype(F32).T
    ssd_out_sum = out_wgrad(ssd_low, order_b).astype(F32).T

    dmixer_t, dvec_t, dstep_t, dlog_t, dtap_x, dtap_b, dskip = ssd_backward(
        *ssd_args, entry, head_gated, local_heads, SP, BLOCK
    )
    dqkv_t = attention_backward(
        qkv_t, rot_t, cosine, sine, run8, log_sums, attn_t, head_attn, local_query, local_keyval, HD, BLOCK, REACH
    )
    dstep_low = dstep_t.astype(BF16)

    partial_normed = (
        mm(dmixer_t, mixer_flat, 0, 1)
        + mm(dvec_t, state_flat, 0, 1)
        + mm(dqkv_t, qkv_flat, 0, 1)
        + mm(dstep_low, step_flat, 0, 1)
    ).astype(BF16)
    sent = lax.dynamic_slice_in_dim(partial_normed, (1 - branch_pos) * half_len, half_len, 0)
    kept = lax.dynamic_slice_in_dim(partial_normed, own_begin, half_len, 0)
    own_grad_normed = kept.astype(F32) + other_branch(sent).astype(F32)
    input_grad = (grad_hidden + rms_back(own_grad_normed, own_rows, own_scale, norm_gain)).astype(
        BF16
    )[None]
    norm_gain_wgrad = jnp.sum(own_grad_normed * own_hat, axis=0)

    def row_sum(partial, order):
        return scatter_sum(
            partial.reshape((row_count, -1) + partial.shape[1:]), row_digits, order
        ).astype(F32)

    def weight_grad(grads_t):
        return mm(full_normed, grads_t, 0, 1).astype(BF16)

    state_part = scatter_sum(owner_rows(weight_grad(dvec_t)), all_digits, order_c)
    state_sum = gather_all(state_part, all_digits, order_c[::-1]).astype(F32)
    gate_sum = row_sum(weight_grad(dmixer_t[:local_inner]), upward)
    mixer_in_sum = row_sum(weight_grad(dmixer_t[local_inner:]), turned)
    qkvs_sum = row_sum(weight_grad(jnp.concatenate([dqkv_t, dstep_low], axis=0)), upward)
    query_cols = local_query * HD
    qkv_cols = dqkv_t.shape[0]
    query_sum = qkvs_sum[:, :query_cols]
    keyval_sum = qkvs_sum[:, query_cols:qkv_cols].reshape((-1,) + keyval_weight.shape[1:])
    step_sum = qkvs_sum[:, qkv_cols : qkv_cols + local_heads]
    mixer_wsum = jnp.stack([gate_sum, mixer_in_sum], axis=1)

    def widen(values):
        full = jnp.zeros(values.shape[:-1] + (2 * values.shape[-1],), F32)
        return lax.dynamic_update_slice_in_dim(
            full, values, branch_pos * values.shape[-1], values.ndim - 1
        )

    heads = slice(0, local_heads)
    small = [
        norm_gain_wgrad,
        ffn_gain_grad,
        dtap_b[:, :4].T,
        dtap_b[:, 4],
        widen(jnp.sum(dstep_t[heads], axis=1)),
        widen(jnp.sum(dlog_t[heads], axis=1) * rates),
        widen(jnp.sum(dskip[:, 0].reshape(local_heads, SP), axis=1)),
        widen(dtap_x[:, :4].T),
        widen(dtap_x[:, 4]),
        ssd_gain_wgrad,
    ]
    flat = jnp.concatenate([item.reshape(-1) for item in small])
    unit = 2 * row_count * 128
    padded = -(-flat.shape[0] // unit) * unit
    flat = jnp.pad(flat, (0, padded - flat.shape[0]))
    flat_part = scatter_sum(flat.reshape(2 * row_count, -1, 128), all_digits, order_c)
    flat_sum = gather_all(flat_part, all_digits, order_c[::-1]).reshape(-1)
    sums = []
    begin = 0
    for item in small:
        sums.append(flat_sum[begin : begin + item.size].reshape(item.shape))
        begin += item.size

    def own_columns(total):
        width = local_inner // row_count
        return lax.dynamic_slice_in_dim(
            total, branch_pos * local_inner + row_pos * width, width, total.ndim - 1
        )

    return (
        block_out,
        input_grad,
        sums[0],
        query_sum,
        keyval_sum,
        mixer_wsum.reshape((-1,) + mixer_weight.shape[1:]),
        state_sum.reshape(state_weight.shape),
        step_sum,
        own_columns(sums[7]),
        sums[2].reshape(conv_state.shape),
        own_columns(sums[8]),
        sums[3].reshape(bias_state.shape),
        sums[4],
        sums[5],
        sums[6],
        own_columns(sums[9]),
        attn_out_sum,
        ssd_out_sum,
        sums[1],
        ffn_grads[0],
        ffn_grads[1],
        ffn_grads[2],
    )


def solution(mesh):
    in_specs = (
        P("rows", "branch", None),
        P("rows", None),
        P(),
        P(None, "branch"),
        P(None, None, "branch"),
        P(None, None, "branch"),
        P(),
        P(None, "branch"),
        P(None, "branch"),
        P(),
        P("branch"),
        P(),
        P("branch"),
        P("branch"),
        P("branch"),
        P("branch"),
        P("branch", None),
        P("branch", None),
        P(),
        P(),
        P(),
        P(),
        P("rows", "branch", None),
    )
    out_specs = (
        P("rows", "branch", None),
        P("rows", "branch", None),
        P(),
        P("rows", "branch"),
        P("rows", None, "branch"),
        P("rows", None, "branch"),
        P(),
        P("rows", "branch"),
        P(None, ("branch", "rows")),
        P(),
        P(("branch", "rows")),
        P(),
        P(),
        P(),
        P(),
        P(("branch", "rows")),
        P("branch", "rows"),
        P("branch", "rows"),
        P(),
        P(None, ("branch", "rows")),
        P(None, ("branch", "rows")),
        P(("branch", "rows"), None),
    )
    return jax.shard_map(
        per_device, mesh=mesh, in_specs=in_specs, out_specs=out_specs, check_vma=False
    )
```

time: 1050 us -> 520 us (0.50)
  local copies, waits for them, and re-layouts: 347 us -> 52.2 us
  matrix products: 233 us -> 46 us
  Pallas kernels: 0 us -> 96.6 us
  other arithmetic: 138 us -> 56.3 us
  waiting for transfers between devices: 227 us -> 180 us
  loops' own time: 11.2 us -> 0 us
    dot_general x112 -> x20, matrix products: 233 us -> 46 us  [mm(): lax.dot_general(left, right, (((left_dim,), (right_dim,)), ((), ())), pre...]
    dynamic_update_slice x32 -> x4, local copies, waits for them, and re-layouts: 180 us -> 1.98 us  [widen(): lax.dynamic_update_slice_in_dim(full, values, branch_pos * values.shape[-...]
    pallas_call x0 -> x6, Pallas kernels: none -> 96.6 us  [the longest x1 34.6 us: ssd_backward(): pl.pallas_call(functools.partial(ssd_backward_kernel, block, heads, head_...]
    ppermute x59 -> x57, waiting for transfers between devices: 180 us -> 136 us  [swap_halves(): return lax.ppermute(values, axis_name, pairs)]
    reduce_sum x16 -> x7, other arithmetic: 33.5 us -> 4.88 us  [the longest x1 2.88 us: per_device(): ffn_gain_grad = jnp.sum(grad_normed_ffn * hidden_hat, axis=0)]
    unnamed x320 -> x154, local copies, waits for them, and re-layouts: 38.6 us -> 12.6 us
    dynamic_slice x31 -> x5, local copies, waits for them, and re-layouts: 27.6 us -> 2.2 us  [the longest x2 1.05 us: own_channels(): return lax.dynamic_slice_in_dim(values, pos * size, size, 0)]
    mul x30 -> x0, other arithmetic: 23.7 us -> none  [the longest x16 8.65 us: advance(): jnp.exp(cumulative[-1]) * carried[-1]]
  transfers between devices with their start and end apart: 63 -> 66, of which waited for: 43 -> 39; matrix products, arithmetic and copies ran while one was open for 43% -> 25% of each run, Pallas kernels for 0% -> 15%
where the time goes in v2:
time: 520 us; the launch traced here: 512 us
  waiting for transfers between devices  180 us (35%)
  Pallas kernels  96.6 us (19%)
  starting transfers between devices  77.4 us (15%)
  other arithmetic  56.3 us (11%)
  local copies, waits for them, and re-layouts  52.2 us (10%)
  matrix products  46 us (9%)
    ppermute x57, waiting for transfers between devices, swap_halves(): return lax.ppermute(values, axis_name, pairs)  136 us
    ppermute x57, starting transfers between devices, swap_halves(): return lax.ppermute(values, axis_name, pairs)  67.5 us
    dot_general x20, matrix products, mm(): lax.dot_general(left, right, (((left_dim,), (right_dim,)), ((), ())), pre...  46 us
    ppermute x9, waiting for transfers between devices, other_branch(): return lax.ppermute(values, 'branch', [(0, 1), (1, 0)])  43.9 us
    pallas_call x1, Pallas kernels, ssd_backward(): pl.pallas_call(functools.partial(ssd_backward_kernel, block, heads, head_...  34.6 us
    convert_element_type x34, other arithmetic, halve(): (kept.astype(jnp.float32) + got.astype(jnp.float32)).astype(values.dtype)  21.4 us
    squeeze x45, local copies, waits for them, and re-layouts, halve(): sent = lax.dynamic_index_in_dim(parts, 1 - my_bit, 1, keepdims=False)  19.7 us
    pallas_call x1, Pallas kernels, feed_forward(): pl.pallas_call(ffn_kernel, grid=(hidden // tile,), in_specs=[pl.BlockSpec...  18.1 us
  transfers between devices with their start and end apart: 66, of which 39 were waited for; matrix products, arithmetic and copies ran while one was open for 25% of the time, Pallas kernels for 15%

profile of v2, /device:TPU:0, one launch (start us, length us, event | category | flops | bytes accessed | tf_op | source)
XLA Modules:
  0.0 511.7 jit_solution(1481637282015363670)
XLA Ops:
  13.2 4.1 copy.326
  20.3 14.3 %collective-permute-done = bf16[512,1024]{1,0:T(8,128)(2,1)S(1)} collective-permute-done((bf16[512,1024]{1,0:T(8,128)(2,1)}, bf16[512,1024]{1,0:T(8,128)(2,1)S(1)}, u32[]{:S(2)}, u32[]{:S(2)}) %collective-permute-start) | collective-permute-done | bytes 1048608 | tf_op jit(solution)/shard_map/ppermute | solution.py:649
  35.2 4.9 fusion.3.z_ref.x_ref.xp_ref
  42.3 15.3 %ssd_forward.1 = (bf16[768,1024]{1,0:T(8,128)(2,1)S(1)}, bf16[4,768,128]{2,1,0:T(8,128)(2,1)S(1)}) custom-call(bf16[1536,1024]{1,0:T(8,128)(2,1)} %fusion.3.z_ref.x_ref.xp_ref, bf16[1536,1024]{1,0:T(8,128)(2,1)} %fusion.3.z_ref.x_ref.xp_ref, bf16[1536,1024]{1,0:T(8,128)(2,1)} %fusion.3.z_ref.x_ref.xp_ref, bf16[256,1024]{1,0:T(8,128)(2,1)S(1)} %fusion.37.b_ref.bp_ref, ...), custom_call_target="tpu_custom_call" | custom-call | flops 1000000000 | bytes 10000000 | tf_op jit(solution)/shard_map/ssd_forward/pallas_call | solution.py:309
  58.8 8.6 %attention_forward.1 = (bf16[256,1024]{1,0:T(8,128)(2,1)S(1)}, bf16[320,1024]{1,0:T(8,128)(2,1)S(1)}, f32[8,1024]{1,0:T(8,128)S(1)}) custom-call(bf16[384,1024]{1,0:T(8,128)(2,1)S(1)} %convolution_convert_fusion.6.proj_ref, f32[32,1024]{1,0:T(8,128)S(1)} %get-tuple-element.298.cos_ref, f32[32,1024]{1,0:T(8,128)S(1)} %get-tuple-element.297.sin_ref, ...), custom_call_target="tpu_custom_call" | custom-call | flops 2000000000 | bytes 10000000 | tf_op jit(solution)/shard_map/attention_forward/pallas_call | solution.py:490
  69.6 10.1 %collective-permute-done.2 = bf16[256,1024]{1,0:T(8,128)(2,1)} collective-permute-done((bf16[256,1024]{1,0:T(8,128)(2,1)}, bf16[256,1024]{1,0:T(8,128)(2,1)}, u32[]{:S(2)}, u32[]{:S(2)}) %collective-permute-start.2) | collective-permute-done | bytes 524320 | tf_op jit(solution)/shard_map/ppermute | solution.py:649
  80.9 19.6 %collective-permute-done.1 = bf16[256,512]{1,0:T(8,128)(2,1)S(1)} collective-permute-done((bf16[256,512]{1,0:T(8,128)(2,1)S(1)}, bf16[256,512]{1,0:T(8,128)(2,1)S(1)}, u32[]{:S(2)}, u32[]{:S(2)}) %collective-permute-start.1) | collective-permute-done | bytes 262176 | tf_op jit(solution)/shard_map/ppermute | solution.py:649
  108.3 18.1 %feed_forward.1 = (f32[512,1024]{1,0:T(8,128)S(1)}, f32[512,1024]{1,0:T(8,128)}, bf16[512,2048]{1,0:T(8,128)(2,1)}, bf16[512,2048]{1,0:T(8,128)(2,1)}, bf16[512,2048]{1,0:T(8,128)(2,1)}) custom-call(bf16[512,1024]{1,0:T(8,128)(2,1)S(1)} %multiply_convert_fusion.1.norm_ref, bf16[512,1024]{1,0:T(8,128)(2,1)S(1)} %bitcast.436, bf16[1024,2048]{1,0:T(8,128)(2,1)} %gate_ref.1, ...), custom_call_target="tpu_custom_call" | custom-call | flops 12884901888 | bytes 30000000 | tf_op jit(solution)/shard_map/feed_forward/pallas_call | solution.py:545
  147.5 9.9 %ffn_wgrads.1 = (bf16[2048,1024]{1,0:T(8,128)(2,1)}, bf16[2048,1024]{1,0:T(8,128)(2,1)}, bf16[2048,1024]{1,0:T(8,128)(2,1)}) custom-call(bf16[512,1024]{1,0:T(8,128)(2,1)S(1)} %multiply_convert_fusion.1.norm_ref, bf16[512,1024]{1,0:T(8,128)(2,1)S(1)} %bitcast.437, bf16[512,2048]{1,0:T(8,128)(2,1)S(1)} %copy-done.1, ...), custom_call_target="tpu_custom_call" | custom-call | flops 6442450944 | bytes 20000000 | tf_op jit(solution)/shard_map/ffn_wgrads/pallas_call | solution.py:586
  157.5 3.3 dynamic-slice_bitcast_fusion.2
  166.0 10.1 %attention_backward.1 = bf16[384,1024]{1,0:T(8,128)(2,1)S(1)} custom-call(bf16[384,1024]{1,0:T(8,128)(2,1)S(1)} %convolution_convert_fusion.6.proj_ref, bf16[320,1024]{1,0:T(8,128)(2,1)S(1)} %get-tuple-element.49.rot_ref, f32[32,1024]{1,0:T(8,128)S(1)} %get-tuple-element.298.cos_ref, f32[32,1024]{1,0:T(8,128)S(1)} %get-tuple-element.297.sin_ref, ...), custom_call_target="tpu_custom_call" | custom-call | flops 5000000000 | bytes 10000000 | tf_op jit(solution)/shard_map/attention_backward/pallas_call | solution.py:505
  181.4 34.6 %ssd_backward.1 = (bf16[1536,1024]{1,0:T(8,128)(2,1)}, bf16[256,1024]{1,0:T(8,128)(2,1)S(1)}, f32[16,1024]{1,0:T(8,128)S(1)}, f32[16,1024]{1,0:T(8,128)S(1)}, f3...) custom-call(bf16[1536,1024]{1,0:T(8,128)(2,1)} %fusion.3.z_ref.x_ref.xp_ref, ...), custom_call_target="tpu_custom_call" | custom-call | flops 3000000000 | bytes 20000000 | tf_op jit(solution)/shard_map/ssd_backward/pallas_call | solution.py:343
  217.6 7.3 %fusion.114 = f32[1024,1024]{1,0:T(8,128)} fusion(bf16[1536,1024]{1,0:T(8,128)(2,1)} %get-tuple-element.47, bf16[1024,1536]{1,0:T(8,128)(2,1)S(1)} %bitcast.466), kind=kOutput, calls=%fused_computation.351 | convolution fusion | flops 3221225472 | bytes 10485760 | tf_op jit(solution)/shard_map/dot_general | solution.py:23
  240.2 3.5 convolution_convert_fusion.5
  254.1 5.1 add_convert_fusion
  272.6 4.3 collective-permute-done.32
  282.6 3.7 collective-permute-done.33
  291.0 3.3 collective-permute-done.45
  308.6 6.0 %collective-permute-done.20 = bf16[4,1,64,400]{3,2,0,1:T(8,128)(2,1)S(1)} collective-permute-done((bf16[4,1,64,400]{3,2,0,1:T(8,128)(2,1)S(1)}, bf16[4,1,64,400]{3,2,0,1:T(8,128)(2,1)S(1)}, u32[]{:S(2)}, u32[]{:S(2)}) %collective-permute-start.20) | collective-permute-done | bytes 204832 | tf_op jit(solution)/shard_map/ppermute | solution.py:605
  315.0 3.8 collective-permute-done.38
  320.7 3.2 collective-permute-done.21
  325.3 3.5 collective-permute-done.39
  364.7 5.9 %collective-permute-done.15 = f32[2,4,128]{2,1,0:T(4,128)S(1)} collective-permute-done((f32[2,4,128]{2,1,0:T(4,128)S(1)}, f32[2,4,128]{2,1,0:T(4,128)S(1)}, u32[]{:S(2)}, u32[]{:S(2)}) %collective-permute-start.15) | collective-permute-done | bytes 4128 | tf_op jit(solution)/shard_map/ppermute | solution.py:605
  378.9 3.6 fusion.41
  399.1 3.5 fusion.2
  420.0 9.0 %collective-permute-done.30 = bf16[1,1,64,768]{3,2,1,0:T(8,128)(2,1)S(1)} collective-permute-done((bf16[1,1,64,768]{3,2,1,0:T(8,128)(2,1)S(1)}, bf16[1,1,64,768]{3,2,1,0:T(8,128)(2,1)S(1)}, u32[]{:S(2)}, u32[]{:S(2)}) %collective-permute-start.30) | collective-permute-done | bytes 98336 | tf_op jit(solution)/shard_map/ppermute | solution.py:605
  429.4 17.8 %collective-permute-done.48 = bf16[2,2,64,768]{3,2,1,0:T(8,128)(2,1)S(1)} collective-permute-done((bf16[2,2,64,768]{3,2,1,0:T(8,128)(2,1)S(1)}, bf16[2,2,64,768]{3,2,1,0:T(8,128)(2,1)S(1)}, u32[]{:S(2)}, u32[]{:S(2)}) %collective-permute-start.48) | collective-permute-done | bytes 393248 | tf_op jit(solution)/shard_map/ppermute | solution.py:605
  448.5 4.5 collective-permute-done.49
  459.0 3.9 collective-permute-start.53
  464.5 15.9 %collective-permute-done.53 = bf16[4,1,64,1024]{3,2,0,1:T(8,128)(2,1)S(1)} collective-permute-done((bf16[4,1,64,1024]{3,2,0,1:T(8,128)(2,1)S(1)}, bf16[4,1,64,1024]{3,2,0,1:T(8,128)(2,1)S(1)}, u32[]{:S(2)}, u32[]{:S(2)}) %collective-permute-start.53) | collective-permute-done | bytes 524320 | tf_op jit(solution)/shard_map/ppermute | solution.py:605
  482.5 12.3 %collective-permute-done.58 = bf16[2,2,64,1024]{3,2,1,0:T(8,128)(2,1)S(1)} collective-permute-done((bf16[2,2,64,1024]{3,2,1,0:T(8,128)(2,1)S(1)}, bf16[2,2,64,1024]{3,2,1,0:T(8,128)(2,1)S(1)}, u32[]{:S(2)}, u32[]{:S(2)}) %collective-permute-start.58) | collective-permute-done | bytes 524320 | tf_op jit(solution)/shard_map/ppermute | solution.py:605
  507.3 3.2 collective-permute-done.65
  (499 shorter events, 232.3 us)
Async XLA Ops:
  0.7 18.9 %collective-permute-start.4 = (f32[768]{0:T(1024)}, f32[768]{0:T(1024)}, u32[]{:S(2)}, u32[]{:S(2)}) collective-permute-start(f32[768]{0:T(1024)} %param.38), channel_id=1, source_target_pairs={{0,16},{16,0},{1,17},{17,1},{2,18},{18,2},{3,19},{19,3},{4,20},{20... | collective-permute-start | bytes 9224 | tf_op jit(solution)/shard_map/ppermute | solution.py:649
  8.3 26.3 %collective-permute-start = (bf16[512,1024]{1,0:T(8,128)(2,1)}, bf16[512,1024]{1,0:T(8,128)(2,1)S(1)}, u32[]{:S(2)}, u32[]{:S(2)}) collective-permute-start(bf16[512,1024]{1,0:T(8,128)(2,1)} %fusion.16), channel_id=1, source_target_pairs={{0,16},{16,0},{1,17},{17,1},{2,18},{18,2},{3,19},{19,3},{4,20},{20... | collective-permute-start | bytes 3145736 | tf_op jit(solution)/shard_map/ppermute | solution.py:649
  8.3 92.4 %collective-permute-start.5 = (bf16[768,1024]{1,0:T(8,128)(2,1)}, bf16[768,1024]{1,0:T(8,128)(2,1)}, u32[]{:S(2)}, u32[]{:S(2)}) collective-permute-start(bf16[768,1024]{1,0:T(8,128)(2,1)} %param.40), channel_id=1, source_target_pairs={{0,16},{16,0},{1,17},{17,1},{2,18},{18,2},{3,19},{19,3},{4,20},{20... | collective-permute-start | bytes 4718600 | tf_op jit(solution)/shard_map/ppermute | solution.py:649
  10.3 69.3 %collective-permute-start.2 = (bf16[256,1024]{1,0:T(8,128)(2,1)}, bf16[256,1024]{1,0:T(8,128)(2,1)}, u32[]{:S(2)}, u32[]{:S(2)}) collective-permute-start(bf16[256,1024]{1,0:T(8,128)(2,1)} %param.39), channel_id=1, source_target_pairs={{0,16},{16,0},{1,17},{17,1},{2,18},{18,2},{3,19},{19,3},{4,20},{20... | collective-permute-start | bytes 1572872 | tf_op jit(solution)/shard_map/ppermute | solution.py:649
  57.7 45.2 %collective-permute-start.3 = (bf16[768,512]{1,0:T(8,128)(2,1)S(1)}, bf16[768,512]{1,0:T(8,128)(2,1)S(1)}, u32[]{:S(2)}, u32[]{:S(2)}) collective-permute-start(bf16[768,512]{1,0:T(8,128)(2,1)S(1)} %constant_dynamic-slice_fusion.27), channel_id=1, source_target_pairs={{0,16},{16,0},{1,17},{17,1},{2,18},{18,2},{3,19},{19,3},{4,20},{20... | collective-permute-start | bytes 2359304 | tf_op jit(solution)/shard_map/ppermute | solution.py:649
  67.5 33.0 %collective-permute-start.1 = (bf16[256,512]{1,0:T(8,128)(2,1)S(1)}, bf16[256,512]{1,0:T(8,128)(2,1)S(1)}, u32[]{:S(2)}, u32[]{:S(2)}) collective-permute-start(bf16[256,512]{1,0:T(8,128)(2,1)S(1)} %constant_dynamic-slice_fusion.28), channel_id=1, source_target_pairs={{0,16},{16,0},{1,17},{17,1},{2,18},{18,2},{3,19},{19,3},{4,20},{20... | collective-permute-start | bytes 786440 | tf_op jit(solution)/shard_map/ppermute | solution.py:649
  140.9 38.8 %collective-permute-start.6 = (bf16[768,512]{1,0:T(8,128)(2,1)}, bf16[768,512]{1,0:T(8,128)(2,1)}, u32[]{:S(2)}, u32[]{:S(2)}) collective-permute-start(bf16[768,512]{1,0:T(8,128)(2,1)} %constant_dynamic-slice_fusion.26), channel_id=1, source_target_pairs={{0,16},{16,0},{1,17},{17,1},{2,18},{18,2},{3,19},{19,3},{4,20},{20... | collective-permute-start | bytes 2359304 | tf_op jit(solution)/shard_map/ppermute | solution.py:649
  141.2 24.6 %collective-permute-start.7 = (bf16[256,512]{1,0:T(8,128)(2,1)S(1)}, bf16[256,512]{1,0:T(8,128)(2,1)S(1)}, u32[]{:S(2)}, u32[]{:S(2)}) collective-permute-start(bf16[256,512]{1,0:T(8,128)(2,1)S(1)} %constant_dynamic-slice_fusion.25), channel_id=1, source_target_pairs={{0,16},{16,0},{1,17},{17,1},{2,18},{18,2},{3,19},{19,3},{4,20},{20... | collective-permute-start | bytes 786440 | tf_op jit(solution)/shard_map/ppermute | solution.py:649
  144.1 32.0 %collective-permute-start.41 = (bf16[16,1,64,256]{3,2,0,1:T(8,128)(2,1)S(1)}, bf16[16,1,64,256]{3,2,0,1:T(8,128)(2,1)}, u32[]{:S(2)}, u32[]{:S(2)}) collective-permute-start(bf16[16,1,64,256]{3,2,0,1:T(8,128)(2,1)S(1)} %dynamic-slice_bitcast_fusion.13), channel_id=1, source_target_pairs={{0,1},{1,0},{2,3},{3,2},{4,5},{5,4},{6,7},{7,6},{8,9},{9,8},{10,11... | collective-permute-start | bytes 1572872 | tf_op jit(solution)/shard_map/ppermute | solution.py:605
  145.7 193.4 %collective-permute-start.46 = (bf16[16,1,64,768]{3,2,0,1:T(8,128)(2,1)}, bf16[16,1,64,768]{3,2,0,1:T(8,128)(2,1)}, u32[]{:S(2)}, u32[]{:S(2)}) collective-permute-start(bf16[16,1,64,768]{3,2,0,1:T(8,128)(2,1)} %dynamic-slice_bitcast_fusion.3), channel_id=1, source_target_pairs={{0,1},{1,0},{2,3},{3,2},{4,5},{5,4},{6,7},{7,6},{8,9},{9,8},{10,11... | collective-permute-start | bytes 4718600 | tf_op jit(solution)/shard_map/ppermute | solution.py:605
  160.8 236.2 %collective-permute-start.51 = (bf16[16,1,64,1024]{3,2,0,1:T(8,128)(2,1)}, bf16[16,1,64,1024]{3,2,0,1:T(8,128)(2,1)}, u32[]{:S(2)}, u32[]{:S(2)}) collective-permute-start(bf16[16,1,64,1024]{3,2,0,1:T(8,128)(2,1)} %dynamic-slice_bitcast_fusion.2), channel_id=1, source_target_pairs={{0,1},{1,0},{2,3},{3,2},{4,5},{5,4},{6,7},{7,6},{8,9},{9,8},{10,11... | collective-permute-start | bytes 6291464 | tf_op jit(solution)/shard_map/ppermute | solution.py:605
  165.8 236.9 %collective-permute-start.56 = (bf16[16,1,64,1024]{3,2,0,1:T(8,128)(2,1)}, bf16[16,1,64,1024]{3,2,0,1:T(8,128)(2,1)}, u32[]{:S(2)}, u32[]{:S(2)}) collective-permute-start(bf16[16,1,64,1024]{3,2,0,1:T(8,128)(2,1)} %dynamic-slice_bitcast_fusion.1), channel_id=1, source_target_pairs={{0,1},{1,0},{2,3},{3,2},{4,5},{5,4},{6,7},{7,6},{8,9},{9,8},{10,11... | collective-permute-start | bytes 6291464 | tf_op jit(solution)/shard_map/ppermute | solution.py:605
  178.2 83.4 %collective-permute-start.42 = (bf16[8,1,64,256]{3,2,0,1:T(8,128)(2,1)}, bf16[8,1,64,256]{3,2,0,1:T(8,128)(2,1)}, u32[]{:S(2)}, u32[]{:S(2)}) collective-permute-start(bf16[8,1,64,256]{3,2,0,1:T(8,128)(2,1)} %dynamic-slice_bitcast_fusion.20), channel_id=1, source_target_pairs={{0,2},{1,3},{2,0},{3,1},{4,6},{5,7},{6,4},{7,5},{8,10},{9,11},{10,... | collective-permute-start | bytes 786440 | tf_op jit(solution)/shard_map/ppermute | solution.py:605
  248.0 51.5 %collective-permute-start.19 = (bf16[8,1,64,400]{3,2,0,1:T(8,128)(2,1)}, bf16[8,1,64,400]{3,2,0,1:T(8,128)(2,1)}, u32[]{:S(2)}, u32[]{:S(2)}) collective-permute-start(bf16[8,1,64,400]{3,2,0,1:T(8,128)(2,1)} %dynamic-slice_bitcast_fusion.14), channel_id=1, source_target_pairs={{0,1},{1,0},{2,3},{3,2},{4,5},{5,4},{6,7},{7,6},{8,9},{9,8},{10,11... | collective-permute-start | bytes 1228808 | tf_op jit(solution)/shard_map/ppermute | solution.py:605
  298.9 37.2 %collective-permute-start.8 = (bf16[512,1024]{1,0:T(8,128)(2,1)}, bf16[512,1024]{1,0:T(8,128)(2,1)}, u32[]{:S(2)}, u32[]{:S(2)}) collective-permute-start(bf16[512,1024]{1,0:T(8,128)(2,1)} %constant_dynamic-slice_fusion.24), channel_id=1, source_target_pairs={{0,16},{16,0},{1,17},{17,1},{2,18},{18,2},{3,19},{19,3},{4,20},{20... | collective-permute-start | bytes 3145736 | tf_op jit(solution)/shard_map/ppermute | solution.py:649
  334.0 73.1 %collective-permute-start.61 = (bf16[16,1,64,1024]{3,2,0,1:T(8,128)(2,1)}, bf16[16,1,64,1024]{3,2,0,1:T(8,128)(2,1)}, u32[]{:S(2)}, u32[]{:S(2)}) collective-permute-start(bf16[16,1,64,1024]{3,2,0,1:T(8,128)(2,1)} %dynamic-slice_bitcast_fusion), channel_id=1, source_target_pairs={{0,1},{1,0},{2,3},{3,2},{4,5},{5,4},{6,7},{7,6},{8,9},{9,8},{10,11... | collective-permute-start | bytes 6291464 | tf_op jit(solution)/shard_map/ppermute | solution.py:605
  346.0 18.3 %collective-permute-start.40 = (bf16[16,32,256]{2,1,0:T(8,128)(2,1)S(1)}, bf16[16,32,256]{2,1,0:T(8,128)(2,1)S(1)}, u32[]{:S(2)}, u32[]{:S(2)}) collective-permute-start(bf16[16,32,256]{2,1,0:T(8,128)(2,1)S(1)} %bitcast.487), channel_id=1, source_target_pairs={{0,1},{1,0},{2,3},{3,2},{4,5},{5,4},{6,7},{7,6},{8,9},{9,8},{10,11... | collective-permute-start | bytes 786440 | tf_op jit(solution)/shard_map/ppermute | solution.py:605
  362.5 25.4 %collective-permute-start.28 = (bf16[2,2,64,768]{3,2,1,0:T(8,128)(2,1)}, bf16[2,2,64,768]{3,2,1,0:T(8,128)(2,1)}, u32[]{:S(2)}, u32[]{:S(2)}) collective-permute-start(bf16[2,2,64,768]{3,2,1,0:T(8,128)(2,1)} %dynamic-slice_bitcast_fusion.16), channel_id=1, source_target_pairs={{0,4},{1,5},{2,6},{3,7},{4,0},{5,1},{6,2},{7,3},{8,12},{9,13},{10,... | collective-permute-start | bytes 1179656 | tf_op jit(solution)/shard_map/ppermute | solution.py:605
  382.5 11.6 %collective-permute-start.24 = (bf16[4,1,64,768]{3,2,0,1:T(8,128)(2,1)S(1)}, bf16[4,1,64,768]{3,2,0,1:T(8,128)(2,1)S(1)}, u32[]{:S(2)}, u32[]{:S(2)}) collective-permute-start(bf16[4,1,64,768]{3,2,0,1:T(8,128)(2,1)S(1)} %copy-done.47), channel_id=1, source_target_pairs={{0,2},{1,3},{2,0},{3,1},{4,6},{5,7},{6,4},{7,5},{8,10},{9,11},{10,... | collective-permute-start | bytes 1179656 | tf_op jit(solution)/shard_map/ppermute | solution.py:605
  387.9 25.8 %collective-permute-start.47 = (bf16[4,2,64,768]{3,2,1,0:T(8,128)(2,1)}, bf16[4,2,64,768]{3,2,1,0:T(8,128)(2,1)S(1)}, u32[]{:S(2)}, u32[]{:S(2)}) collective-permute-start(bf16[4,2,64,768]{3,2,1,0:T(8,128)(2,1)} %dynamic-slice_bitcast_fusion.7), channel_id=1, source_target_pairs={{0,4},{1,5},{2,6},{3,7},{4,0},{5,1},{6,2},{7,3},{8,12},{9,13},{10,... | collective-permute-start | bytes 2359304 | tf_op jit(solution)/shard_map/ppermute | solution.py:605
  394.1 17.9 %collective-permute-start.29 = (bf16[1,2,64,768]{3,2,1,0:T(8,128)(2,1)S(1)}, bf16[1,2,64,768]{3,2,1,0:T(8,128)(2,1)S(1)}, u32[]{:S(2)}, u32[]{:S(2)}) collective-permute-start(bf16[1,2,64,768]{3,2,1,0:T(8,128)(2,1)S(1)} %constant_dynamic-slice_fusion.11), channel_id=1, source_target_pairs={{0,8},{1,9},{2,10},{3,11},{4,12},{5,13},{6,14},{7,15},{8,0},{9,1},... | collective-permute-start | bytes 589832 | tf_op jit(solution)/shard_map/ppermute | solution.py:605
  397.0 19.9 %collective-permute-start.25 = (bf16[2,1,64,768]{3,2,0,1:T(8,128)(2,1)S(1)}, bf16[2,1,64,768]{3,2,0,1:T(8,128)(2,1)S(1)}, u32[]{:S(2)}, u32[]{:S(2)}) collective-permute-start(bf16[2,1,64,768]{3,2,0,1:T(8,128)(2,1)S(1)} %dynamic-slice_bitcast_fusion.23), channel_id=1, source_target_pairs={{0,4},{1,5},{2,6},{3,7},{4,0},{5,1},{6,2},{7,3},{8,12},{9,13},{10,... | collective-permute-start | bytes 589832 | tf_op jit(solution)/shard_map/ppermute | solution.py:605
  402.7 55.8 %collective-permute-start.52 = (bf16[8,1,64,1024]{3,2,0,1:T(8,128)(2,1)S(1)}, bf16[8,1,64,1024]{3,2,0,1:T(8,128)(2,1)S(1)}, u32[]{:S(2)}, u32[]{:S(2)}) collective-permute-start(bf16[8,1,64,1024]{3,2,0,1:T(8,128)(2,1)S(1)} %dynamic-slice_bitcast_fusion.6), channel_id=1, source_target_pairs={{0,2},{1,3},{2,0},{3,1},{4,6},{5,7},{6,4},{7,5},{8,10},{9,11},{10,... | collective-permute-start | bytes 3145736 | tf_op jit(solution)/shard_map/ppermute | solution.py:605
  407.1 55.8 %collective-permute-start.57 = (bf16[4,2,64,1024]{3,2,1,0:T(8,128)(2,1)S(1)}, bf16[4,2,64,1024]{3,2,1,0:T(8,128)(2,1)S(1)}, u32[]{:S(2)}, u32[]{:S(2)}) collective-permute-start(bf16[4,2,64,1024]{3,2,1,0:T(8,128)(2,1)S(1)} %dynamic-slice_bitcast_fusion.5), channel_id=1, source_target_pairs={{0,4},{1,5},{2,6},{3,7},{4,0},{5,1},{6,2},{7,3},{8,12},{9,13},{10,... | collective-permute-start | bytes 3145736 | tf_op jit(solution)/shard_map/ppermute | solution.py:605
  412.0 51.4 %collective-permute-start.62 = (bf16[1,8,64,1024]{3,2,1,0:T(8,128)(2,1)S(1)}, bf16[1,8,64,1024]{3,2,1,0:T(8,128)(2,1)S(1)}, u32[]{:S(2)}, u32[]{:S(2)}) collective-permute-start(bf16[1,8,64,1024]{3,2,1,0:T(8,128)(2,1)S(1)} %dynamic-slice_bitcast_fusion.4), channel_id=1, source_target_pairs={{0,16},{16,0},{1,17},{17,1},{2,18},{18,2},{3,19},{19,3},{4,20},{20... | collective-permute-start | bytes 3145736 | tf_op jit(solution)/shard_map/ppermute | solution.py:605
  413.8 15.3 %collective-permute-start.30 = (bf16[1,1,64,768]{3,2,1,0:T(8,128)(2,1)S(1)}, bf16[1,1,64,768]{3,2,1,0:T(8,128)(2,1)S(1)}, u32[]{:S(2)}, u32[]{:S(2)}) collective-permute-start(bf16[1,1,64,768]{3,2,1,0:T(8,128)(2,1)S(1)} %constant_dynamic-slice_fusion.10), channel_id=1, source_target_pairs={{0,2},{1,3},{2,0},{3,1},{4,6},{5,7},{6,4},{7,5},{8,10},{9,11},{10,... | collective-permute-start | bytes 294920 | tf_op jit(solution)/shard_map/ppermute | solution.py:605
  416.9 30.2 %collective-permute-start.48 = (bf16[2,2,64,768]{3,2,1,0:T(8,128)(2,1)S(1)}, bf16[2,2,64,768]{3,2,1,0:T(8,128)(2,1)S(1)}, u32[]{:S(2)}, u32[]{:S(2)}) collective-permute-start(bf16[2,2,64,768]{3,2,1,0:T(8,128)(2,1)S(1)} %dynamic-slice_bitcast_fusion.15), channel_id=1, source_target_pairs={{0,8},{1,9},{2,10},{3,11},{4,12},{5,13},{6,14},{7,15},{8,0},{9,1},... | collective-permute-start | bytes 1179656 | tf_op jit(solution)/shard_map/ppermute | solution.py:605
  429.1 19.5 %collective-permute-start.26 = (bf16[1,1,64,768]{3,2,0,1:T(8,128)(2,1)S(1)}, bf16[1,1,64,768]{3,2,0,1:T(8,128)(2,1)S(1)}, u32[]{:S(2)}, u32[]{:S(2)}) collective-permute-start(bf16[1,1,64,768]{3,2,0,1:T(8,128)(2,1)S(1)} %constant_dynamic-slice_fusion.12), channel_id=1, source_target_pairs={{0,8},{1,9},{2,10},{3,11},{4,12},{5,13},{6,14},{7,15},{8,0},{9,1},... | collective-permute-start | bytes 294920 | tf_op jit(solution)/shard_map/ppermute | solution.py:605
  459.0 21.4 %collective-permute-start.53 = (bf16[4,1,64,1024]{3,2,0,1:T(8,128)(2,1)S(1)}, bf16[4,1,64,1024]{3,2,0,1:T(8,128)(2,1)S(1)}, u32[]{:S(2)}, u32[]{:S(2)}) collective-permute-start(bf16[4,1,64,1024]{3,2,0,1:T(8,128)(2,1)S(1)} %dynamic-slice_bitcast_fusion.12), channel_id=1, source_target_pairs={{0,4},{1,5},{2,6},{3,7},{4,0},{5,1},{6,2},{7,3},{8,12},{9,13},{10,... | collective-permute-start | bytes 1572872 | tf_op jit(solution)/shard_map/ppermute | solution.py:605
  463.3 31.4 %collective-permute-start.58 = (bf16[2,2,64,1024]{3,2,1,0:T(8,128)(2,1)S(1)}, bf16[2,2,64,1024]{3,2,1,0:T(8,128)(2,1)S(1)}, u32[]{:S(2)}, u32[]{:S(2)}) collective-permute-start(bf16[2,2,64,1024]{3,2,1,0:T(8,128)(2,1)S(1)} %dynamic-slice_bitcast_fusion.11), channel_id=1, source_target_pairs={{0,8},{1,9},{2,10},{3,11},{4,12},{5,13},{6,14},{7,15},{8,0},{9,1},... | collective-permute-start | bytes 1572872 | tf_op jit(solution)/shard_map/ppermute | solution.py:605
  463.9 31.7 %collective-permute-start.63 = (bf16[4,1,64,1024]{3,2,0,1:T(8,128)(2,1)S(1)}, bf16[4,1,64,1024]{3,2,0,1:T(8,128)(2,1)S(1)}, u32[]{:S(2)}, u32[]{:S(2)}) collective-permute-start(bf16[4,1,64,1024]{3,2,0,1:T(8,128)(2,1)S(1)} %dynamic-slice_bitcast_fusion.10), channel_id=1, source_target_pairs={{0,2},{1,3},{2,0},{3,1},{4,6},{5,7},{6,4},{7,5},{8,10},{9,11},{10,... | collective-permute-start | bytes 1572872 | tf_op jit(solution)/shard_map/ppermute | solution.py:605
  480.6 16.9 %collective-permute-start.54 = (bf16[2,1,64,1024]{3,2,0,1:T(8,128)(2,1)S(1)}, bf16[2,1,64,1024]{3,2,0,1:T(8,128)(2,1)S(1)}, u32[]{:S(2)}, u32[]{:S(2)}) collective-permute-start(bf16[2,1,64,1024]{3,2,0,1:T(8,128)(2,1)S(1)} %dynamic-slice_bitcast_fusion.19), channel_id=1, source_target_pairs={{0,8},{1,9},{2,10},{3,11},{4,12},{5,13},{6,14},{7,15},{8,0},{9,1},... | collective-permute-start | bytes 786440 | tf_op jit(solution)/shard_map/ppermute | solution.py:605
  (109 other events, 906.1 us)
